TPU v7x, 512 devices: a whole 4x8x8 slice. The times are simulated.
512 devices in a mesh: blk: 32 (over x, z_hi, core), col: 16 (over y, z_lo).
Axes of the slice: x: 4, y: 8, z: 8 (z_hi: 4, z_lo: 2; z = z_hi * 2 + z_lo), core: 2. Of those that a mesh axis runs over, the one named last changes fastest.
Arguments:
- samples: bfloat16 [8192, 768], P('blk'), may hold values from -3 to 3
- targets: float32 [8192, 256], P('blk'), may hold values from -6 to 6
- batch_index: int32 [4096], P('blk'), may hold values from 0 to 255
- centers: bfloat16 [65536, 768], P(('blk', 'col')), may hold values from -3 to 3
- weights: float32 [65536, 256], P(('blk', 'col')), may hold values from -6 to 6
- nystrom_index: int32 [1536], replicated, may hold values from 0 to 65535, as said below
- eigvecs: float32 [1536, 128], replicated, may hold values from -0.15625 to 0.15625
- coefficient: float32 [128], replicated, may hold values from 0.4 to 0.95
Outputs:
- residual: float32 [4096, 256], P(('blk', 'col'))
- new_weights: float32 [65536, 256], P(('blk', 'col'))
Inputs may be any that keep to these rules, and one draw needn't show every extreme that they name: Batch row i is sample row (i // 128) * 256 + batch_index[i]. `nystrom_index`: 1536 distinct center rows.
All inputs are finite; a program needn't handle non-finite values.
Results may differ from a plain program's by a relative error of at most 0.0003.
The roundings to bfloat16 on the way count: a program that leaves them out, or rounds other values in their place, can miss the bound.
Values may be sent and summed in bfloat16 or wider, within the bound.
A program may use at most 64 MiB of HBM per device.

v0:
```python
import jax
import jax.numpy as jnp
from jax import lax
from jax.sharding import PartitionSpec as P

spread = 1.0
shift_sq = 1.0
step_size = 4.0


def shifted(block, axis, distance):
    devices = range(lax.axis_size(axis))
    route = [((i - distance) % len(devices), i) for i in devices]
    return lax.ppermute(block, axis, route)


def copy_for_each(x, axis):
    peers = lax.axis_size(axis)
    return lax.all_to_all(jnp.broadcast_to(x[None], (peers, *x.shape)), axis, 0, 0, tiled=True)


def over_copies(x, axis):
    return copy_for_each(x, axis).sum(axis=0)


def kernel_block(points, centers, center_sq):
    point_sq = jnp.sum(jnp.square(points.astype(jnp.float32)), axis=1, keepdims=True)
    cross = lax.dot_general(
        points, centers, (((1,), (1,)), ((), ())), preferred_element_type=jnp.float32
    )
    dist_sq = point_sq + center_sq[None, :] - 2.0 * cross
    return jnp.exp(-jnp.sqrt(dist_sq + shift_sq) / spread).astype(jnp.bfloat16)


def move_up(points_now):
    return shifted(points_now, "blk", 1)


def pass_up(partial_value):
    return shifted(partial_value, "blk", 1)


def local(samples, targets, batch_index, centers, weights, nystrom_index, eigvecs, coefficient):
    blocks = lax.axis_size("blk")
    columns = lax.axis_size("col")
    my_block = lax.axis_index("blk")
    blk_rows = batch_index.shape[0]
    n_center = centers.shape[0]
    out_width = weights.shape[1]
    points = jnp.take(samples, batch_index, axis=0)
    wanted = jnp.take(targets, batch_index, axis=0)
    center_sq = jnp.sum(jnp.square(centers.astype(jnp.float32)), axis=1)
    weights_low = weights.astype(jnp.bfloat16)
    kernel_store = jnp.zeros((blocks * blk_rows, n_center), jnp.bfloat16)

    def absorb(points_now, partial_value, stored, offset):
        kernel = kernel_block(points_now, centers, center_sq)
        stored = lax.dynamic_update_slice(stored, kernel, (offset, 0))
        return (
            partial_value + jnp.dot(kernel, weights_low, preferred_element_type=jnp.float32),
            stored,
        )

    def walk_step(step_idx, state_now):
        points_now, partial_value, stored = state_now
        partial_value, stored = absorb(
            points_now, partial_value, stored, (my_block - step_idx) % blocks * blk_rows
        )
        return (move_up(points_now), pass_up(partial_value), stored)

    initial = (points, jnp.zeros((blk_rows, out_width), jnp.float32), kernel_store)
    points_now, partial_value, kernel_store = lax.fori_loop(0, blocks - 1, walk_step, initial)
    partial_value, kernel_store = absorb(
        points_now, partial_value, kernel_store, (my_block + 1) % blocks * blk_rows
    )
    partial_value = pass_up(partial_value)
    share_rows = blk_rows // columns
    prediction = over_copies(partial_value, "col")
    residual_full = prediction - wanted
    gathered = lax.all_gather(residual_full.astype(jnp.bfloat16), "blk", axis=0, tiled=True)
    own_resid = lax.dynamic_slice_in_dim(
        residual_full, lax.axis_index("col") * share_rows, share_rows, 0
    )
    gradient = lax.dot_general(
        kernel_store, gathered, (((0,), (0,)), ((), ())), preferred_element_type=jnp.float32
    )
    first_row = lax.axis_index(("blk", "col")) * n_center
    position = nystrom_index - first_row
    inside = (position >= 0) & (position < n_center)
    position = jnp.where(inside, position, n_center)
    target_row = jnp.minimum(position, n_center - 1)
    picked = jnp.where(inside[:, None], jnp.take(gradient, target_row, axis=0), 0.0)
    highest = lax.Precision.HIGHEST
    local_proj = lax.dot_general(eigvecs, picked, (((0,), (0,)), ((), ())), precision=highest)
    projected = lax.psum(local_proj, ("blk", "col"))
    correction = jnp.dot(eigvecs, coefficient[:, None] * projected, precision=highest)
    adjusted = gradient.at[position].add(-correction, mode="drop")
    return (own_resid, weights - step_size * adjusted)


def solution(mesh):
    in_specs = (
        P("blk", None),
        P("blk", None),
        P("blk"),
        P(("blk", "col"), None),
        P(("blk", "col"), None),
        P(),
        P(),
        P(),
    )
    out_specs = (P(("blk", "col"), None), P(("blk", "col"), None))
    return jax.shard_map(local, mesh=mesh, in_specs=in_specs, out_specs=out_specs, check_vma=False)
```

profile of v0, /device:TPU:1, one launch (start us, length us, event | category | flops | bytes accessed | tf_op | source)
XLA Modules:
  0.0 877.6 jit_solution(8725641700618093670)
XLA Ops:
  12.9 442.6 %while.19 = (s32[]{:T(128)}, bf16[128,768]{1,0:T(8,128)(2,1)S(1)}, f32[128,256]{1,0:T(8,128)S(1)}, bf16[4096,128]{1,0:T(8,128)(2,1)S(1)}, f32[128]{0:T(128)S(1)}...) while((s32[]{:T(128)}, bf16[128,768]{1,0:T(8,128)(2,1)S(1)}, ...), condition=%wide.region_3.4_spmd, body=%wide.region_1.3_spmd.sunk | while | flops 33980304 | bytes 2721664 | solution.py:72
  114.4 10.1 %collective-permute-done.1 = f32[128,256]{1,0:T(8,128)S(1)} collective-permute-done((f32[128,256]{1,0:T(8,128)S(1)}, f32[128,256]{1,0:T(8,128)S(1)}, u32[]{:S(2)}, u32[]{:S(2)}) %collective-permute-start.1) | collective-permute-done | bytes 131104 | tf_op jit(solution)/shard_map/while/body/eval_jaxpr/ppermute | solution.py:14
  143.1 10.1 %collective-permute-done.1 = f32[128,256]{1,0:T(8,128)S(1)} collective-permute-done((f32[128,256]{1,0:T(8,128)S(1)}, f32[128,256]{1,0:T(8,128)S(1)}, u32[]{:S(2)}, u32[]{:S(2)}) %collective-permute-start.1) | collective-permute-done | bytes 131104 | tf_op jit(solution)/shard_map/while/body/eval_jaxpr/ppermute | solution.py:14
  171.9 10.0 %collective-permute-done.1 = f32[128,256]{1,0:T(8,128)S(1)} collective-permute-done((f32[128,256]{1,0:T(8,128)S(1)}, f32[128,256]{1,0:T(8,128)S(1)}, u32[]{:S(2)}, u32[]{:S(2)}) %collective-permute-start.1) | collective-permute-done | bytes 131104 | tf_op jit(solution)/shard_map/while/body/eval_jaxpr/ppermute | solution.py:14
  200.7 10.0 %collective-permute-done.1 = f32[128,256]{1,0:T(8,128)S(1)} collective-permute-done((f32[128,256]{1,0:T(8,128)S(1)}, f32[128,256]{1,0:T(8,128)S(1)}, u32[]{:S(2)}, u32[]{:S(2)}) %collective-permute-start.1) | collective-permute-done | bytes 131104 | tf_op jit(solution)/shard_map/while/body/eval_jaxpr/ppermute | solution.py:14
  215.1 10.0 %collective-permute-done.1 = f32[128,256]{1,0:T(8,128)S(1)} collective-permute-done((f32[128,256]{1,0:T(8,128)S(1)}, f32[128,256]{1,0:T(8,128)S(1)}, u32[]{:S(2)}, u32[]{:S(2)}) %collective-permute-start.1) | collective-permute-done | bytes 131104 | tf_op jit(solution)/shard_map/while/body/eval_jaxpr/ppermute | solution.py:14
  229.5 10.0 %collective-permute-done.1 = f32[128,256]{1,0:T(8,128)S(1)} collective-permute-done((f32[128,256]{1,0:T(8,128)S(1)}, f32[128,256]{1,0:T(8,128)S(1)}, u32[]{:S(2)}, u32[]{:S(2)}) %collective-permute-start.1) | collective-permute-done | bytes 131104 | tf_op jit(solution)/shard_map/while/body/eval_jaxpr/ppermute | solution.py:14
  243.9 10.0 %collective-permute-done.1 = f32[128,256]{1,0:T(8,128)S(1)} collective-permute-done((f32[128,256]{1,0:T(8,128)S(1)}, f32[128,256]{1,0:T(8,128)S(1)}, u32[]{:S(2)}, u32[]{:S(2)}) %collective-permute-start.1) | collective-permute-done | bytes 131104 | tf_op jit(solution)/shard_map/while/body/eval_jaxpr/ppermute | solution.py:14
  258.3 10.0 %collective-permute-done.1 = f32[128,256]{1,0:T(8,128)S(1)} collective-permute-done((f32[128,256]{1,0:T(8,128)S(1)}, f32[128,256]{1,0:T(8,128)S(1)}, u32[]{:S(2)}, u32[]{:S(2)}) %collective-permute-start.1) | collective-permute-done | bytes 131104 | tf_op jit(solution)/shard_map/while/body/eval_jaxpr/ppermute | solution.py:14
  272.7 10.0 %collective-permute-done.1 = f32[128,256]{1,0:T(8,128)S(1)} collective-permute-done((f32[128,256]{1,0:T(8,128)S(1)}, f32[128,256]{1,0:T(8,128)S(1)}, u32[]{:S(2)}, u32[]{:S(2)}) %collective-permute-start.1) | collective-permute-done | bytes 131104 | tf_op jit(solution)/shard_map/while/body/eval_jaxpr/ppermute | solution.py:14
  287.1 10.0 %collective-permute-done.1 = f32[128,256]{1,0:T(8,128)S(1)} collective-permute-done((f32[128,256]{1,0:T(8,128)S(1)}, f32[128,256]{1,0:T(8,128)S(1)}, u32[]{:S(2)}, u32[]{:S(2)}) %collective-permute-start.1) | collective-permute-done | bytes 131104 | tf_op jit(solution)/shard_map/while/body/eval_jaxpr/ppermute | solution.py:14
  301.5 10.0 %collective-permute-done.1 = f32[128,256]{1,0:T(8,128)S(1)} collective-permute-done((f32[128,256]{1,0:T(8,128)S(1)}, f32[128,256]{1,0:T(8,128)S(1)}, u32[]{:S(2)}, u32[]{:S(2)}) %collective-permute-start.1) | collective-permute-done | bytes 131104 | tf_op jit(solution)/shard_map/while/body/eval_jaxpr/ppermute | solution.py:14
  315.9 10.0 %collective-permute-done.1 = f32[128,256]{1,0:T(8,128)S(1)} collective-permute-done((f32[128,256]{1,0:T(8,128)S(1)}, f32[128,256]{1,0:T(8,128)S(1)}, u32[]{:S(2)}, u32[]{:S(2)}) %collective-permute-start.1) | collective-permute-done | bytes 131104 | tf_op jit(solution)/shard_map/while/body/eval_jaxpr/ppermute | solution.py:14
  344.7 10.0 %collective-permute-done.1 = f32[128,256]{1,0:T(8,128)S(1)} collective-permute-done((f32[128,256]{1,0:T(8,128)S(1)}, f32[128,256]{1,0:T(8,128)S(1)}, u32[]{:S(2)}, u32[]{:S(2)}) %collective-permute-start.1) | collective-permute-done | bytes 131104 | tf_op jit(solution)/shard_map/while/body/eval_jaxpr/ppermute | solution.py:14
  359.1 10.0 %collective-permute-done.1 = f32[128,256]{1,0:T(8,128)S(1)} collective-permute-done((f32[128,256]{1,0:T(8,128)S(1)}, f32[128,256]{1,0:T(8,128)S(1)}, u32[]{:S(2)}, u32[]{:S(2)}) %collective-permute-start.1) | collective-permute-done | bytes 131104 | tf_op jit(solution)/shard_map/while/body/eval_jaxpr/ppermute | solution.py:14
  387.9 10.0 %collective-permute-done.1 = f32[128,256]{1,0:T(8,128)S(1)} collective-permute-done((f32[128,256]{1,0:T(8,128)S(1)}, f32[128,256]{1,0:T(8,128)S(1)}, u32[]{:S(2)}, u32[]{:S(2)}) %collective-permute-start.1) | collective-permute-done | bytes 131104 | tf_op jit(solution)/shard_map/while/body/eval_jaxpr/ppermute | solution.py:14
  402.3 10.0 %collective-permute-done.1 = f32[128,256]{1,0:T(8,128)S(1)} collective-permute-done((f32[128,256]{1,0:T(8,128)S(1)}, f32[128,256]{1,0:T(8,128)S(1)}, u32[]{:S(2)}, u32[]{:S(2)}) %collective-permute-start.1) | collective-permute-done | bytes 131104 | tf_op jit(solution)/shard_map/while/body/eval_jaxpr/ppermute | solution.py:14
  431.1 10.0 %collective-permute-done.1 = f32[128,256]{1,0:T(8,128)S(1)} collective-permute-done((f32[128,256]{1,0:T(8,128)S(1)}, f32[128,256]{1,0:T(8,128)S(1)}, u32[]{:S(2)}, u32[]{:S(2)}) %collective-permute-start.1) | collective-permute-done | bytes 131104 | tf_op jit(solution)/shard_map/while/body/eval_jaxpr/ppermute | solution.py:14
  445.5 10.0 %collective-permute-done.1 = f32[128,256]{1,0:T(8,128)S(1)} collective-permute-done((f32[128,256]{1,0:T(8,128)S(1)}, f32[128,256]{1,0:T(8,128)S(1)}, u32[]{:S(2)}, u32[]{:S(2)}) %collective-permute-start.1) | collective-permute-done | bytes 131104 | tf_op jit(solution)/shard_map/while/body/eval_jaxpr/ppermute | solution.py:14
  457.9 10.0 %collective-permute-done.2 = f32[128,256]{1,0:T(8,128)S(1)} collective-permute-done((f32[128,256]{1,0:T(8,128)S(1)}, f32[128,256]{1,0:T(8,128)S(1)}, u32[]{:S(2)}, u32[]{:S(2)}) %collective-permute-start.2) | collective-permute-done | bytes 131104 | tf_op jit(solution)/shard_map/ppermute | solution.py:14
  469.4 10.9 %all-to-all-start = ((f32[16,128,256]{2,1,0:T(8,128)}), f32[16,128,256]{2,1,0:T(8,128)S(1)}, u32[]{:S(2)}, u32[]{:S(2)}) async-start(f32[16,128,256]{2,1,0:T(8,128)} %broadcast_in_dim.78), calls=%async_computation | async-start | bytes 4194304 | tf_op jit(solution)/shard_map/all_to_all | solution.py:19
  481.2 41.0 %all-to-all-done = f32[16,128,256]{2,1,0:T(8,128)S(1)} async-done(((f32[16,128,256]{2,1,0:T(8,128)}), f32[16,128,256]{2,1,0:T(8,128)S(1)}, u32[]{:S(2)}, u32[]{:S(2)}) %all-to-all-start) | async-done | bytes 2097184 | tf_op jit(solution)/shard_map/all_to_all | solution.py:19
  523.2 61.6 %all-gather.2.cloned.1.call-done = bf16[4096,256]{1,0:T(8,128)(2,1)} async-done(((bf16[128,256]{1,0:T(8,128)(2,1)}), bf16[4096,256]{1,0:T(8,128)(2,1)}) %all-gather.2.cloned.1.call-update) | async-done | bytes 2097168 | tf_op jit(solution)/shard_map/all_gather | solution.py:80
  594.2 261.6 %all-reduce.2.cloned.1.call-done = f32[128,256]{1,0:T(8,128)} async-done(((f32[128,256]{1,0:T(8,128)}), f32[128,256]{1,0:T(8,128)}) %all-reduce.2.cloned.1.call-update) | async-done | bytes 131088 | tf_op jit(solution)/shard_map/psum | solution.py:95
  (276 shorter events, 297.1 us)
Async XLA Ops:
  51.4 16.2 %collective-permute-start = (bf16[128,768]{1,0:T(8,128)(2,1)S(1)}, bf16[128,768]{1,0:T(8,128)(2,1)S(1)}, u32[]{:S(2)}, u32[]{:S(2)}) collective-permute-start(bf16[128,768]{1,0:T(8,128)(2,1)S(1)} %copy.18), channel_id=1, source_target_pairs={{496,0},{0,16},{16,32},{32,48},{48,64},{64,80},{80,96},{96,112},{1... | collective-permute-start | bytes 589832 | tf_op jit(solution)/shard_map/while/body/eval_jaxpr/ppermute | solution.py:14
  109.7 14.9 %collective-permute-start = (bf16[128,768]{1,0:T(8,128)(2,1)S(1)}, bf16[128,768]{1,0:T(8,128)(2,1)S(1)}, u32[]{:S(2)}, u32[]{:S(2)}) collective-permute-start(bf16[128,768]{1,0:T(8,128)(2,1)S(1)} %copy.18), channel_id=1, source_target_pairs={{496,0},{0,16},{16,32},{32,48},{48,64},{64,80},{80,96},{96,112},{1... | collective-permute-start | bytes 589832 | tf_op jit(solution)/shard_map/while/body/eval_jaxpr/ppermute | solution.py:14
  138.7 14.5 %collective-permute-start = (bf16[128,768]{1,0:T(8,128)(2,1)S(1)}, bf16[128,768]{1,0:T(8,128)(2,1)S(1)}, u32[]{:S(2)}, u32[]{:S(2)}) collective-permute-start(bf16[128,768]{1,0:T(8,128)(2,1)S(1)} %copy.18), channel_id=1, source_target_pairs={{496,0},{0,16},{16,32},{32,48},{48,64},{64,80},{80,96},{96,112},{1... | collective-permute-start | bytes 589832 | tf_op jit(solution)/shard_map/while/body/eval_jaxpr/ppermute | solution.py:14
  167.5 14.4 %collective-permute-start = (bf16[128,768]{1,0:T(8,128)(2,1)S(1)}, bf16[128,768]{1,0:T(8,128)(2,1)S(1)}, u32[]{:S(2)}, u32[]{:S(2)}) collective-permute-start(bf16[128,768]{1,0:T(8,128)(2,1)S(1)} %copy.18), channel_id=1, source_target_pairs={{496,0},{0,16},{16,32},{32,48},{48,64},{64,80},{80,96},{96,112},{1... | collective-permute-start | bytes 589832 | tf_op jit(solution)/shard_map/while/body/eval_jaxpr/ppermute | solution.py:14
  196.3 14.4 %collective-permute-start = (bf16[128,768]{1,0:T(8,128)(2,1)S(1)}, bf16[128,768]{1,0:T(8,128)(2,1)S(1)}, u32[]{:S(2)}, u32[]{:S(2)}) collective-permute-start(bf16[128,768]{1,0:T(8,128)(2,1)S(1)} %copy.18), channel_id=1, source_target_pairs={{496,0},{0,16},{16,32},{32,48},{48,64},{64,80},{80,96},{96,112},{1... | collective-permute-start | bytes 589832 | tf_op jit(solution)/shard_map/while/body/eval_jaxpr/ppermute | solution.py:14
  210.7 14.4 %collective-permute-start = (bf16[128,768]{1,0:T(8,128)(2,1)S(1)}, bf16[128,768]{1,0:T(8,128)(2,1)S(1)}, u32[]{:S(2)}, u32[]{:S(2)}) collective-permute-start(bf16[128,768]{1,0:T(8,128)(2,1)S(1)} %copy.18), channel_id=1, source_target_pairs={{496,0},{0,16},{16,32},{32,48},{48,64},{64,80},{80,96},{96,112},{1... | collective-permute-start | bytes 589832 | tf_op jit(solution)/shard_map/while/body/eval_jaxpr/ppermute | solution.py:14
  225.1 14.4 %collective-permute-start = (bf16[128,768]{1,0:T(8,128)(2,1)S(1)}, bf16[128,768]{1,0:T(8,128)(2,1)S(1)}, u32[]{:S(2)}, u32[]{:S(2)}) collective-permute-start(bf16[128,768]{1,0:T(8,128)(2,1)S(1)} %copy.18), channel_id=1, source_target_pairs={{496,0},{0,16},{16,32},{32,48},{48,64},{64,80},{80,96},{96,112},{1... | collective-permute-start | bytes 589832 | tf_op jit(solution)/shard_map/while/body/eval_jaxpr/ppermute | solution.py:14
  239.5 14.4 %collective-permute-start = (bf16[128,768]{1,0:T(8,128)(2,1)S(1)}, bf16[128,768]{1,0:T(8,128)(2,1)S(1)}, u32[]{:S(2)}, u32[]{:S(2)}) collective-permute-start(bf16[128,768]{1,0:T(8,128)(2,1)S(1)} %copy.18), channel_id=1, source_target_pairs={{496,0},{0,16},{16,32},{32,48},{48,64},{64,80},{80,96},{96,112},{1... | collective-permute-start | bytes 589832 | tf_op jit(solution)/shard_map/while/body/eval_jaxpr/ppermute | solution.py:14
  253.9 14.4 %collective-permute-start = (bf16[128,768]{1,0:T(8,128)(2,1)S(1)}, bf16[128,768]{1,0:T(8,128)(2,1)S(1)}, u32[]{:S(2)}, u32[]{:S(2)}) collective-permute-start(bf16[128,768]{1,0:T(8,128)(2,1)S(1)} %copy.18), channel_id=1, source_target_pairs={{496,0},{0,16},{16,32},{32,48},{48,64},{64,80},{80,96},{96,112},{1... | collective-permute-start | bytes 589832 | tf_op jit(solution)/shard_map/while/body/eval_jaxpr/ppermute | solution.py:14
  268.3 14.4 %collective-permute-start = (bf16[128,768]{1,0:T(8,128)(2,1)S(1)}, bf16[128,768]{1,0:T(8,128)(2,1)S(1)}, u32[]{:S(2)}, u32[]{:S(2)}) collective-permute-start(bf16[128,768]{1,0:T(8,128)(2,1)S(1)} %copy.18), channel_id=1, source_target_pairs={{496,0},{0,16},{16,32},{32,48},{48,64},{64,80},{80,96},{96,112},{1... | collective-permute-start | bytes 589832 | tf_op jit(solution)/shard_map/while/body/eval_jaxpr/ppermute | solution.py:14
  282.7 14.4 %collective-permute-start = (bf16[128,768]{1,0:T(8,128)(2,1)S(1)}, bf16[128,768]{1,0:T(8,128)(2,1)S(1)}, u32[]{:S(2)}, u32[]{:S(2)}) collective-permute-start(bf16[128,768]{1,0:T(8,128)(2,1)S(1)} %copy.18), channel_id=1, source_target_pairs={{496,0},{0,16},{16,32},{32,48},{48,64},{64,80},{80,96},{96,112},{1... | collective-permute-start | bytes 589832 | tf_op jit(solution)/shard_map/while/body/eval_jaxpr/ppermute | solution.py:14
  297.1 14.4 %collective-permute-start = (bf16[128,768]{1,0:T(8,128)(2,1)S(1)}, bf16[128,768]{1,0:T(8,128)(2,1)S(1)}, u32[]{:S(2)}, u32[]{:S(2)}) collective-permute-start(bf16[128,768]{1,0:T(8,128)(2,1)S(1)} %copy.18), channel_id=1, source_target_pairs={{496,0},{0,16},{16,32},{32,48},{48,64},{64,80},{80,96},{96,112},{1... | collective-permute-start | bytes 589832 | tf_op jit(solution)/shard_map/while/body/eval_jaxpr/ppermute | solution.py:14
  311.5 14.4 %collective-permute-start = (bf16[128,768]{1,0:T(8,128)(2,1)S(1)}, bf16[128,768]{1,0:T(8,128)(2,1)S(1)}, u32[]{:S(2)}, u32[]{:S(2)}) collective-permute-start(bf16[128,768]{1,0:T(8,128)(2,1)S(1)} %copy.18), channel_id=1, source_target_pairs={{496,0},{0,16},{16,32},{32,48},{48,64},{64,80},{80,96},{96,112},{1... | collective-permute-start | bytes 589832 | tf_op jit(solution)/shard_map/while/body/eval_jaxpr/ppermute | solution.py:14
  325.9 14.4 %collective-permute-start = (bf16[128,768]{1,0:T(8,128)(2,1)S(1)}, bf16[128,768]{1,0:T(8,128)(2,1)S(1)}, u32[]{:S(2)}, u32[]{:S(2)}) collective-permute-start(bf16[128,768]{1,0:T(8,128)(2,1)S(1)} %copy.18), channel_id=1, source_target_pairs={{496,0},{0,16},{16,32},{32,48},{48,64},{64,80},{80,96},{96,112},{1... | collective-permute-start | bytes 589832 | tf_op jit(solution)/shard_map/while/body/eval_jaxpr/ppermute | solution.py:14
  340.3 14.4 %collective-permute-start = (bf16[128,768]{1,0:T(8,128)(2,1)S(1)}, bf16[128,768]{1,0:T(8,128)(2,1)S(1)}, u32[]{:S(2)}, u32[]{:S(2)}) collective-permute-start(bf16[128,768]{1,0:T(8,128)(2,1)S(1)} %copy.18), channel_id=1, source_target_pairs={{496,0},{0,16},{16,32},{32,48},{48,64},{64,80},{80,96},{96,112},{1... | collective-permute-start | bytes 589832 | tf_op jit(solution)/shard_map/while/body/eval_jaxpr/ppermute | solution.py:14
  354.7 14.4 %collective-permute-start = (bf16[128,768]{1,0:T(8,128)(2,1)S(1)}, bf16[128,768]{1,0:T(8,128)(2,1)S(1)}, u32[]{:S(2)}, u32[]{:S(2)}) collective-permute-start(bf16[128,768]{1,0:T(8,128)(2,1)S(1)} %copy.18), channel_id=1, source_target_pairs={{496,0},{0,16},{16,32},{32,48},{48,64},{64,80},{80,96},{96,112},{1... | collective-permute-start | bytes 589832 | tf_op jit(solution)/shard_map/while/body/eval_jaxpr/ppermute | solution.py:14
  369.1 14.4 %collective-permute-start = (bf16[128,768]{1,0:T(8,128)(2,1)S(1)}, bf16[128,768]{1,0:T(8,128)(2,1)S(1)}, u32[]{:S(2)}, u32[]{:S(2)}) collective-permute-start(bf16[128,768]{1,0:T(8,128)(2,1)S(1)} %copy.18), channel_id=1, source_target_pairs={{496,0},{0,16},{16,32},{32,48},{48,64},{64,80},{80,96},{96,112},{1... | collective-permute-start | bytes 589832 | tf_op jit(solution)/shard_map/while/body/eval_jaxpr/ppermute | solution.py:14
  383.5 14.4 %collective-permute-start = (bf16[128,768]{1,0:T(8,128)(2,1)S(1)}, bf16[128,768]{1,0:T(8,128)(2,1)S(1)}, u32[]{:S(2)}, u32[]{:S(2)}) collective-permute-start(bf16[128,768]{1,0:T(8,128)(2,1)S(1)} %copy.18), channel_id=1, source_target_pairs={{496,0},{0,16},{16,32},{32,48},{48,64},{64,80},{80,96},{96,112},{1... | collective-permute-start | bytes 589832 | tf_op jit(solution)/shard_map/while/body/eval_jaxpr/ppermute | solution.py:14
  397.9 14.4 %collective-permute-start = (bf16[128,768]{1,0:T(8,128)(2,1)S(1)}, bf16[128,768]{1,0:T(8,128)(2,1)S(1)}, u32[]{:S(2)}, u32[]{:S(2)}) collective-permute-start(bf16[128,768]{1,0:T(8,128)(2,1)S(1)} %copy.18), channel_id=1, source_target_pairs={{496,0},{0,16},{16,32},{32,48},{48,64},{64,80},{80,96},{96,112},{1... | collective-permute-start | bytes 589832 | tf_op jit(solution)/shard_map/while/body/eval_jaxpr/ppermute | solution.py:14
  426.7 14.4 %collective-permute-start = (bf16[128,768]{1,0:T(8,128)(2,1)S(1)}, bf16[128,768]{1,0:T(8,128)(2,1)S(1)}, u32[]{:S(2)}, u32[]{:S(2)}) collective-permute-start(bf16[128,768]{1,0:T(8,128)(2,1)S(1)} %copy.18), channel_id=1, source_target_pairs={{496,0},{0,16},{16,32},{32,48},{48,64},{64,80},{80,96},{96,112},{1... | collective-permute-start | bytes 589832 | tf_op jit(solution)/shard_map/while/body/eval_jaxpr/ppermute | solution.py:14
  441.1 14.4 %collective-permute-start = (bf16[128,768]{1,0:T(8,128)(2,1)S(1)}, bf16[128,768]{1,0:T(8,128)(2,1)S(1)}, u32[]{:S(2)}, u32[]{:S(2)}) collective-permute-start(bf16[128,768]{1,0:T(8,128)(2,1)S(1)} %copy.18), channel_id=1, source_target_pairs={{496,0},{0,16},{16,32},{32,48},{48,64},{64,80},{80,96},{96,112},{1... | collective-permute-start | bytes 589832 | tf_op jit(solution)/shard_map/while/body/eval_jaxpr/ppermute | solution.py:14
  469.4 52.8 %all-to-all-start = ((f32[16,128,256]{2,1,0:T(8,128)}), f32[16,128,256]{2,1,0:T(8,128)S(1)}, u32[]{:S(2)}, u32[]{:S(2)}) async-start(f32[16,128,256]{2,1,0:T(8,128)} %broadcast_in_dim.78), calls=%async_computation | async-start | bytes 4194304 | tf_op jit(solution)/shard_map/all_to_all | solution.py:19
  480.4 104.4 %all-gather.2.cloned.1.call-start = ((), (), s32[]{:S(2)}) async-start(), calls=%async_computation.1 | async-start | bytes 2162688 | tf_op jit(solution)/shard_map/all_gather | solution.py:80
  523.1 332.6 %all-reduce.2.cloned.1.call-start = ((), (), s32[]{:S(2)}) async-start(), calls=%async_computation.2 | async-start | bytes 262144 | tf_op jit(solution)/shard_map/psum | solution.py:95
  (49 other events, 1424.2 us)
Sparse Core Ops, SparseCore 0:
  523.2 61.5 all-gather.1
  593.7 262.0 all-reduce.1
where the time goes:
time: 880 us; the launch traced here: 878 us
  waiting for transfers between devices  652 us (74%)
  starting transfers between devices  159 us (18%)
  matrix products  21.7 us (2%)
  other arithmetic  17.7 us (2%)
  between operations  14.3 us (2%)
  local copies, waits for them, and re-layouts  11.1 us (1%)
    ppermute x63, waiting for transfers between devices, shifted(): return lax.ppermute(block, axis, route)  288 us
    psum x1, waiting for transfers between devices, local(): projected = lax.psum(local_proj, ('blk', 'col'))  262 us
    ppermute x63, starting transfers between devices, shifted(): return lax.ppermute(block, axis, route)  148 us
    all_gather x1, waiting for transfers between devices, local(): lax.all_gather(residual_full.astype(jnp.bfloat16), 'blk', axis=0, tiled=T...  61.6 us
    all_to_all x1, waiting for transfers between devices, copy_for_each(): lax.all_to_all(jnp.broadcast_to(x[None], (peers, *x.shape)), axis, 0, 0,...  41 us
  transfers between devices with their start and end apart: 66, of which 35 were waited for; matrix products, arithmetic and copies ran while one was open for 2% of the time, Pallas kernels for 0%

commit v1 on v0

v1 whole, which is shorter than its diff:
```python
import jax
import jax.numpy as jnp
from jax import lax
from jax.experimental import pallas as pl
from jax.experimental.pallas import tpu as pltpu
from jax.sharding import PartitionSpec as P

MESH = pl.DeviceIdType.MESH
F32, BF16 = jnp.float32, jnp.bfloat16

shift_sq = 1.0
step_size = 4.0

NX, NY, NZ, NH = 4, 8, 8, 4
RUN = 8
ROWS = 128
CHUNKS = 4


def spot(x, y, z, core):
    return (x * 8 + (z // 2) * 2 + core, y * 2 + z % 2)


def send(src, dst, send_sem, recv_sem, where):
    return pltpu.make_async_remote_copy(
        src_ref=src, dst_ref=dst, send_sem=send_sem, recv_sem=recv_sem, device_id=where, device_id_type=MESH
    )


def split3(v):
    a = v.astype(BF16)
    rest = v - a.astype(F32)
    b = rest.astype(BF16)
    c = (rest - b.astype(F32)).astype(BF16)
    return a, b, c


def nt(a, b):
    return lax.dot_general(a, b, (((1,), (1,)), ((), ())), preferred_element_type=F32)


def body(
    samples, targets, idx_row, centers, weights, nys, eig, coef, out_res, out_w,
    samp, targ, idx_v, idx_s, nys_v, eig_v, coef_v, wts,
    pts, cw, e123, ecat, csq, kmat, part, rec1, red1, rec2, rall, mall, gpart, grec, gs, gx,
    ld, zs, zr, xs, xr, cs, cr, s1, r1, s2, r2, gs1, gr1, gs2, gr2, ds, dr, dxs, dxr,
):
    blk, col = lax.axis_index("blk"), lax.axis_index("col")
    x, h, core = blk // 8, (blk // 2) % 4, blk % 2
    y, low = col // 2, col % 2
    z = 2 * h + low
    other = 1 - core

    def at_y(k):
        return spot(x, (y + k) % NY, z, core)

    def at_z(k):
        return spot(x, y, (z + k) % NZ, core)

    def at_x(k):
        return spot((x + k) % NX, y, z, core)

    partner = spot(x, y, z, other)

    barrier = pltpu.get_barrier_semaphore()

    def greet(k, carry):
        pl.semaphore_signal(barrier, inc=1, device_id=at_y(k), device_id_type=MESH)
        pl.semaphore_signal(barrier, inc=1, device_id=at_z(k), device_id_type=MESH)
        return carry

    lax.fori_loop(1, 8, greet, 0)
    for k in (1, 2, 3):
        pl.semaphore_signal(barrier, inc=1, device_id=at_x(k), device_id_type=MESH)
    pl.semaphore_signal(barrier, inc=1, device_id=partner, device_id_type=MESH)

    mine = core * 4 + x
    loads = [
        pltpu.make_async_copy(idx_row, idx_v, ld.at[0]),
        pltpu.make_async_copy(samples, samp, ld.at[1]),
        pltpu.make_async_copy(centers, cw.at[mine, :, pl.ds(0, 768)], ld.at[2]),
        pltpu.make_async_copy(weights, wts, ld.at[3]),
        pltpu.make_async_copy(nys, nys_v, ld.at[4]),
        pltpu.make_async_copy(eig, eig_v, ld.at[5]),
        pltpu.make_async_copy(coef, coef_v, ld.at[6]),
        pltpu.make_async_copy(targets, targ, ld.at[7]),
        pltpu.make_async_copy(idx_row, idx_s, ld.at[8]),
    ]
    for copy in loads:
        copy.start()
    for copy in loads[:4]:
        copy.wait()

    chosen = jnp.where(lax.broadcasted_iota(jnp.int32, (256, ROWS), 0) == idx_v[...], 1.0, 0.0).astype(F32)
    own = jnp.dot(chosen.T.astype(BF16), samp[...], preferred_element_type=F32)
    own = own.reshape(NY, 2, RUN, 768)
    own = jnp.concatenate([own[:, 0].reshape(64, 768), own[:, 1].reshape(64, 768)], axis=0)
    pts[h] = own.astype(BF16)
    cw[mine, :, 768:] = wts[...].astype(BF16)

    pl.semaphore_wait(barrier, 18)

    outward = 2 * low - 1
    zo, zi = spot(x, y, (z + outward + NZ) % NZ, core), spot(x, y, (z - outward + NZ) % NZ, core)
    h_a = ((z + outward + NZ) % NZ) // 2
    h_b = ((z - 2 * outward + NZ) % NZ) // 2
    h_c = ((z + 3 * outward + NZ) % NZ) // 2
    step = ROWS // CHUNKS

    def zpiece(block, kind, i, where):
        piece = pts.at[block, pl.ds(i * step, step), :]
        return send(piece, piece, zs.at[kind, i], zr.at[kind, i], where)

    x_next, x_prev, x_far = (x + 1) % NX, (x + 3) % NX, (x + 2) % NX
    right, left = at_x(1), at_x(3)

    def half(block_x, part_no, sem, where):
        piece = cw.at[core * 4 + block_x, pl.ds(part_no * 64, 64), :]
        return send(piece, piece, xs.at[sem], xr.at[sem], where)

    def across(block_core, block_x, sem):
        piece = cw.at[block_core * 4 + block_x]
        return send(piece, piece, cs.at[sem], cr.at[sem], partner)

    for i in range(CHUNKS):
        zpiece(h, 0, i, zo).start()
    half(x, 0, 0, right).start()
    half(x, 1, 1, left).start()
    half(x, 1, 2, right).start()
    half(x, 0, 3, left).start()
    across(core, x, 0).start()

    for copy in loads[4:]:
        copy.wait()
    e1, e2, e3 = split3(eig_v[...])
    e123[:, 0:128] = e1
    e123[:, 128:256] = e2
    e123[:, 256:384] = e3

    def eig_rows(j, carry):
        owner = ((j % 4) * 8 + h * 2 + j // 4) * 16 + col
        place = lax.broadcasted_iota(jnp.int32, (ROWS, 1536), 0) + owner * ROWS
        hit = jnp.where(place == nys_v[...], 1.0, 0.0).astype(BF16)
        ecat[j] = jnp.dot(hit, e123[...], preferred_element_type=F32).astype(BF16)
        return carry

    def relay_a(i):
        zpiece(h_a, 0, i, zo).wait_recv()
        zpiece(h_a, 1, i, zi).start()

    def relay_b(i):
        zpiece(h_b, 1, i, zi).wait_recv()
        zpiece(h_b, 2, i, zo).start()

    relay_a(0)
    relay_a(1)
    half(x_prev, 0, 0, right).wait_recv()
    half(x_prev, 0, 4, right).start()
    half(x_next, 1, 1, left).wait_recv()
    half(x_next, 1, 5, left).start()
    relay_b(0)
    relay_a(2)
    relay_b(1)
    relay_a(3)
    relay_b(2)
    half(x_prev, 1, 2, right).wait_recv()
    across(core, x_prev, 1).start()
    half(x_next, 0, 3, left).wait_recv()
    across(core, x_next, 2).start()
    relay_b(3)
    lax.fori_loop(0, 8, eig_rows, 0)
    half(x_far, 0, 4, right).wait_recv()
    half(x_far, 1, 5, left).wait_recv()
    across(core, x_far, 3).start()
    for i in range(CHUNKS):
        zpiece(h_c, 2, i, zo).wait_recv()
    across(other, x, 0).wait_recv()
    across(other, x_prev, 1).wait_recv()
    across(other, x_next, 2).wait_recv()
    across(other, x_far, 3).wait_recv()

    def norms(j, carry):
        c = cw[j, :, 0:768].astype(F32)
        total = jnp.sum(c * c, axis=1, keepdims=True)
        csq[j] = jnp.broadcast_to(total, (ROWS, ROWS)).T[0:8, :]
        return carry

    lax.fori_loop(0, 8, norms, 0)

    def tile(t, carry):
        p = pts[t]
        p32 = p.astype(F32)
        psq = jnp.sum(p32 * p32, axis=1, keepdims=True)
        for half_no in range(2):
            cen = cw[half_no * 4:half_no * 4 + 4, :, 0:768].reshape(512, 768)
            cross = nt(p, cen)
            row = jnp.concatenate([csq[half_no * 4 + i, 0:1, :] for i in range(4)], axis=1)
            dist = psq + row - 2.0 * cross
            kmat[t, :, half_no * 512:half_no * 512 + 512] = jnp.exp(-jnp.sqrt(dist + shift_sq)).astype(BF16)
        k = kmat[t]
        pred = jnp.dot(k, cw[:, :, 768:].reshape(1024, 256), preferred_element_type=F32)
        m = jnp.dot(k, ecat[...].reshape(1024, 384), preferred_element_type=F32)
        m = m[:, 0:128] + m[:, 128:256] + m[:, 256:384]
        rows = pl.ds(2 * t, 2)
        part[0, rows] = pred[:, 0:128].reshape(2, 8, RUN, 128)
        part[1, rows] = pred[:, 128:256].reshape(2, 8, RUN, 128)
        part[2, rows] = m.reshape(2, 8, RUN, 128)
        return carry

    lax.fori_loop(0, NH, tile, 0)

    def first(stream, k):
        if stream == 0:
            return send(part.at[0, :, (y + k) % NY], rec1.at[0, k], s1.at[0, k], r1.at[0, k], at_y(k))
        return send(part.at[stream, (z + k) % NZ], rec1.at[stream, k], s1.at[stream, k], r1.at[stream, k], at_z(k))

    def second(stream, k):
        if stream == 0:
            return send(red1.at[0, (z + k) % NZ], rec2.at[0, k], s2.at[0, k], r2.at[0, k], at_z(k))
        return send(red1.at[stream, (y + k) % NY], rec2.at[stream, k], s2.at[stream, k], r2.at[stream, k], at_y(k))

    def start_first(k, carry):
        for stream in range(3):
            first(stream, k).start()
        return carry

    lax.fori_loop(1, 8, start_first, 0)

    def finish_first(stream):
        own = part[0, :, y] if stream == 0 else part[stream, z]
        red1[stream] = own

        def add(k, carry):
            first(stream, k).wait_recv()
            red1[stream] += rec1[stream, k]
            return carry

        lax.fori_loop(1, 8, add, 0)

        def go(k, carry):
            second(stream, k).start()
            return carry

        lax.fori_loop(1, 8, go, 0)

    def finish_second(stream):
        def add(k, total):
            second(stream, k).wait_recv()
            return total + rec2[stream, k]

        return lax.fori_loop(1, 8, add, red1[stream, z if stream == 0 else y])

    finish_first(0)
    finish_first(1)
    finish_first(2)
    lo = finish_second(0)
    hi = finish_second(1)

    for r in range(RUN):
        row = idx_s[0, col * RUN + r]
        out_res[r:r + 1, :] = targ[pl.ds(row, 1), :]
    out_res[:, 0:128] = lo - out_res[:, 0:128]
    out_res[:, 128:256] = hi - out_res[:, 128:256]
    rall[z, y] = out_res[...].astype(BF16)

    def r_first(k, src_y):
        return send(rall.at[z, src_y], rall.at[z, src_y], gs1.at[0, k], gr1.at[0, k], at_y(k))

    def r_second(k, src_z):
        return send(rall.at[src_z], rall.at[src_z], gs2.at[0, k], gr2.at[0, k], at_z(k))

    def m_first(k, src_z):
        return send(mall.at[src_z, y], mall.at[src_z, y], gs1.at[1, k], gr1.at[1, k], at_z(k))

    def m_second(k, src_y):
        return send(mall.at[:, src_y], mall.at[:, src_y], gs2.at[1, k], gr2.at[1, k], at_y(k))

    def loop8(fn):
        def run(k, carry):
            fn(k)
            return carry

        lax.fori_loop(1, 8, run, 0)

    loop8(lambda k: r_first(k, y).start())
    mall[z, y] = finish_second(2)
    loop8(lambda k: m_first(k, z).start())
    loop8(lambda k: r_first(k, (y - k + NY) % NY).wait_recv())
    loop8(lambda k: r_second(k, z).start())
    loop8(lambda k: m_first(k, (z - k + NZ) % NZ).wait_recv())
    loop8(lambda k: m_second(k, y).start())
    loop8(lambda k: r_second(k, (z - k + NZ) % NZ).wait_recv())
    loop8(lambda k: m_second(k, (y - k + NY) % NY).wait_recv())

    resid = rall[...].astype(F32).reshape(512, 256)
    resid_t = resid.T.astype(BF16)
    m1, m2, m3 = split3(mall[...].reshape(512, 128))
    proj = (
        jnp.dot(resid_t, m1, preferred_element_type=F32)
        + jnp.dot(resid_t, m2, preferred_element_type=F32)
        + jnp.dot(resid_t, m3, preferred_element_type=F32)
    )
    a1, a2, a3 = split3(proj * coef_v[...])
    a_one = jnp.concatenate([a1, a1, a1], axis=1)
    a_two = jnp.concatenate([a2, a2], axis=1)

    def grad(i, carry):
        j = 4 * jnp.where(i < 4, other, core) + i % 4
        rows = pl.ds(pl.multiple_of(j * ROWS, ROWS), ROWS)
        km = kmat[:, :, rows].reshape(512, ROWS)
        e = ecat[j]
        g = jnp.dot(resid_t, km, preferred_element_type=F32)
        g = g - (nt(a_one, e) + nt(a_two, e[:, 0:256]) + nt(a3, e[:, 0:128]))
        gpart[j] = g
        return carry

    def swap(i):
        return send(gpart.at[other * 4 + i], grec.at[i], ds.at[i], dr.at[i], partner)

    lax.fori_loop(0, 4, grad, 0)
    for i in range(4):
        swap(i).start()
    lax.fori_loop(4, 8, grad, 0)

    def to_x(k):
        return send(gs.at[(x + k) % NX], gx.at[k], dxs.at[k], dxr.at[k], at_x(k))

    for i in range(4):
        swap(i).wait_recv()
        gs[i] = gpart[core * 4 + i] + grec[i]
    for k in (2, 1, 3):
        to_x(k).start()
    total = gs[x]
    for k in (1, 3, 2):
        to_x(k).wait_recv()
        total = total + gx[k]
    out_w[...] = wts[...] - step_size * total.T

    for i in range(CHUNKS):
        zpiece(h, 0, i, zo).wait_send()
        zpiece(h_a, 1, i, zi).wait_send()
        zpiece(h_b, 2, i, zo).wait_send()
    for i in range(6):
        half(x, 0, i, right).wait_send()
    for i in range(4):
        across(core, x, i).wait_send()
        swap(i).wait_send()
    for k in (1, 2, 3):
        to_x(k).wait_send()

    def drain(k):
        for stream in range(3):
            first(stream, k).wait_send()
            second(stream, k).wait_send()
        r_first(k, y).wait_send()
        r_second(k, z).wait_send()
        m_first(k, z).wait_send()
        m_second(k, y).wait_send()

    loop8(drain)


def local(samples, targets, batch_index, centers, weights, nystrom_index, eigvecs, coefficient):
    dma = pltpu.SemaphoreType.DMA
    vm = pltpu.VMEM
    return pl.pallas_call(
        body,
        out_shape=(jax.ShapeDtypeStruct((RUN, 256), F32), jax.ShapeDtypeStruct((ROWS, 256), F32)),
        in_specs=[pl.BlockSpec(memory_space=pl.ANY)] * 8,
        out_specs=(pl.BlockSpec(memory_space=pltpu.VMEM), pl.BlockSpec(memory_space=pltpu.VMEM)),
        scratch_shapes=[
            vm((256, 768), BF16), vm((256, 256), F32), vm((1, 128), jnp.int32), pltpu.SMEM((1, 128), jnp.int32),
            vm((1, 1536), jnp.int32), vm((1536, 128), F32), vm((1, 128), F32), vm((ROWS, 256), F32),
            vm((NH, ROWS, 768), BF16), vm((8, ROWS, 1024), BF16), vm((1536, 384), BF16), vm((8, ROWS, 384), BF16),
            vm((8, 8, ROWS), F32), vm((NH, ROWS, 1024), BF16),
            vm((3, 8, 8, RUN, 128), F32), vm((3, 8, 8, RUN, 128), F32), vm((3, 8, RUN, 128), F32),
            vm((3, 8, RUN, 128), F32), vm((8, 8, RUN, 256), BF16), vm((8, 8, RUN, 128), F32),
            vm((8, 256, ROWS), F32), vm((4, 256, ROWS), F32), vm((4, 256, ROWS), F32), vm((4, 256, ROWS), F32),
            dma((9,)), dma((3, CHUNKS)), dma((3, CHUNKS)), dma((6,)), dma((6,)), dma((4,)), dma((4,)),
            dma((3, 8)), dma((3, 8)), dma((3, 8)), dma((3, 8)),
            dma((2, 8)), dma((2, 8)), dma((2, 8)), dma((2, 8)), dma((4,)), dma((4,)), dma((4,)), dma((4,)),
        ],
        compiler_params=pltpu.CompilerParams(collective_id=0, has_side_effects=True, vmem_limit_bytes=48 << 20),
        name="step",
    )(
        samples, targets, batch_index.reshape(1, 128), centers, weights, nystrom_index.reshape(1, 1536),
        eigvecs, coefficient.reshape(1, 128),
    )


def solution(mesh):
    in_specs = (
        P("blk", None),
        P("blk", None),
        P("blk"),
        P(("blk", "col"), None),
        P(("blk", "col"), None),
        P(),
        P(),
        P(),
    )
    out_specs = (P(("blk", "col"), None), P(("blk", "col"), None))
    return jax.shard_map(local, mesh=mesh, in_specs=in_specs, out_specs=out_specs, check_vma=False)
```

time: 880 us -> 90.1 us (0.10)
  waiting for transfers between devices: 652 us -> 0 us
  starting transfers between devices: 159 us -> 0 us
  Pallas kernels: 0 us -> 82.3 us
  matrix products: 21.7 us -> 0 us
  other arithmetic: 17.7 us -> 0 us
  between operations: 14.3 us -> 0.67 us
    ppermute x63 -> x0, waiting for transfers between devices: 288 us -> none  [shifted(): return lax.ppermute(block, axis, route)]
    psum x1 -> x0, waiting for transfers between devices: 262 us -> none  [local(): projected = lax.psum(local_proj, ('blk', 'col'))]
    ppermute x63 -> x0, starting transfers between devices: 148 us -> none  [shifted(): return lax.ppermute(block, axis, route)]
    pallas_call x0 -> x1, Pallas kernels: none -> 82.3 us  [local(): pl.pallas_call(body, out_shape=(jax.ShapeDtypeStruct((RUN, 256), F32), ja...]
    all_gather x1 -> x0, waiting for transfers between devices: 61.6 us -> none  [local(): lax.all_gather(residual_full.astype(jnp.bfloat16), 'blk', axis=0, tiled=T...]
    all_to_all x1 -> x0, waiting for transfers between devices: 41 us -> none  [copy_for_each(): lax.all_to_all(jnp.broadcast_to(x[None], (peers, *x.shape)), axis, 0, 0,...]
    dot_general x67 -> x0, matrix products: 21.7 us -> none  [the longest x32 8.24 us: kernel_block(): lax.dot_general(points, centers, (((1,), (1,)), ((), ())), preferred_elem...]
    all_to_all x1 -> x0, starting transfers between devices: 10.9 us -> none  [copy_for_each(): lax.all_to_all(jnp.broadcast_to(x[None], (peers, *x.shape)), axis, 0, 0,...]
  transfers between devices with their start and end apart: 66 -> 0, of which waited for: 35 -> 0; matrix products, arithmetic and copies ran while one was open for 2% -> 0% of each run, Pallas kernels for 0% -> 0%
where the time goes in v1:
time: 90.1 us; the launch traced here: 89.8 us
  Pallas kernels  82.3 us (91%)
  local copies, waits for them, and re-layouts  6.88 us (8%)
    pallas_call x1, Pallas kernels, local(): pl.pallas_call(body, out_shape=(jax.ShapeDtypeStruct((RUN, 256), F32), ja...  82.3 us
    unnamed x16, local copies, waits for them, and re-layouts  6.17 us

profile of v1, /device:TPU:1, one launch (start us, length us, event | category | flops | bytes accessed | tf_op | source)
XLA Modules:
  0.0 89.8 jit_solution(10199745453295452373)
XLA Ops:
  0.6 0.0 copy-start.5
  0.6 0.0 copy-start.6
  0.7 0.7 reshape.14.nys
  1.4 0.0 copy-done.5
  1.4 0.0 copy-done.6
  1.4 0.0 copy-start
  1.4 1.1 %copy-done = f32[1536,128]{1,0:T(8,128)S(1)} copy-done((f32[1536,128]{1,0:T(8,128)S(1)}, f32[1536,128]{1,0:T(8,128)}, u32[]{:S(2)}) %copy-start) | copy-done | bytes 786456
  2.5 0.0 copy-start.1
  2.5 1.0 %copy-done.1 = bf16[256,768]{1,0:T(8,128)(2,1)S(1)} copy-done((bf16[256,768]{1,0:T(8,128)(2,1)S(1)}, bf16[256,768]{1,0:T(8,128)(2,1)}, u32[]{:S(2)}) %copy-start.1) | copy-done | bytes 393240
  3.5 0.0 copy-start.2
  3.5 0.9 %copy-done.2 = f32[256,256]{1,0:T(8,128)S(1)} copy-done((f32[256,256]{1,0:T(8,128)S(1)}, f32[256,256]{1,0:T(8,128)}, u32[]{:S(2)}) %copy-start.2) | copy-done | bytes 262168
  4.5 0.0 copy-start.3
  4.5 0.9 %copy-done.3 = bf16[128,768]{1,0:T(8,128)(2,1)S(1)} copy-done((bf16[128,768]{1,0:T(8,128)(2,1)S(1)}, bf16[128,768]{1,0:T(8,128)(2,1)}, u32[]{:S(2)}) %copy-start.3) | copy-done | bytes 196632
  5.4 0.0 copy-start.4
  5.4 0.9 %copy-done.4 = f32[128,256]{1,0:T(8,128)S(1)} copy-done((f32[128,256]{1,0:T(8,128)S(1)}, f32[128,256]{1,0:T(8,128)}, u32[]{:S(2)}) %copy-start.4) | copy-done | bytes 131096
  6.3 82.3 %step.1 = (f32[8,256]{1,0:T(8,128)S(1)}, f32[128,256]{1,0:T(8,128)S(1)}) custom-call(bf16[256,768]{1,0:T(8,128)(2,1)S(1)} %copy-done.1, f32[256,256]{1,0:T(8,128)S(1)} %copy-done.2, s32[1,128]{1,0:T(1,128)S(1)} %bitcast.2, bf16[128,768]{1,0:T(8,128)(2,1)S(1)} %copy-done.3, f32[128,256]{1,0:T(8,128)S(1)} %copy-done.4, s32[1,1536]{1,0:T(1,128)S(1)} %reshape.14.nys, ...), custom_call_target="tpu_custom_call" | custom-call | tf_op jit(solution)/shard_map/step/pallas_call | solution.py:366
  88.6 0.6 copy.12
  89.2 0.7 copy.13
Async XLA Ops:
  0.6 0.7 copy-start.5
  0.6 0.7 copy-start.6
  1.4 1.1 %copy-start = (f32[1536,128]{1,0:T(8,128)S(1)}, f32[1536,128]{1,0:T(8,128)}, u32[]{:S(2)}) copy-start(f32[1536,128]{1,0:T(8,128)} %eig.1) | copy-start | bytes 2359300
  2.5 1.0 %copy-start.1 = (bf16[256,768]{1,0:T(8,128)(2,1)S(1)}, bf16[256,768]{1,0:T(8,128)(2,1)}, u32[]{:S(2)}) copy-start(bf16[256,768]{1,0:T(8,128)(2,1)} %samples.1) | copy-start | bytes 1179652
  3.5 0.9 %copy-start.2 = (f32[256,256]{1,0:T(8,128)S(1)}, f32[256,256]{1,0:T(8,128)}, u32[]{:S(2)}) copy-start(f32[256,256]{1,0:T(8,128)} %targets.1) | copy-start | bytes 786436
  4.5 0.9 %copy-start.3 = (bf16[128,768]{1,0:T(8,128)(2,1)S(1)}, bf16[128,768]{1,0:T(8,128)(2,1)}, u32[]{:S(2)}) copy-start(bf16[128,768]{1,0:T(8,128)(2,1)} %centers.1) | copy-start | bytes 589828
  5.4 0.9 %copy-start.4 = (f32[128,256]{1,0:T(8,128)S(1)}, f32[128,256]{1,0:T(8,128)}, u32[]{:S(2)}) copy-start(f32[128,256]{1,0:T(8,128)} %weights.1) | copy-start | bytes 393220

commit v2 on v0

v2 whole, which is shorter than its diff:
```python
import jax
import jax.numpy as jnp
from jax import lax
from jax.experimental import pallas as pl
from jax.experimental.pallas import tpu as pltpu
from jax.sharding import PartitionSpec as P

MESH = pl.DeviceIdType.MESH
F32, BF16 = jnp.float32, jnp.bfloat16

shift_sq = 1.0
step_size = 4.0

NX, NY, NZ, NH = 4, 8, 8, 4
RUN = 8
ROWS = 128
STAGE = 9


def spot(x, y, z, core):
    return (x * 8 + (z // 2) * 2 + core, y * 2 + z % 2)


def send(src, dst, sems, where):
    return pltpu.make_async_remote_copy(
        src_ref=src, dst_ref=dst, send_sem=sems[0], recv_sem=sems[1], device_id=where, device_id_type=MESH
    )


def split3(v):
    a = v.astype(BF16)
    rest = v - a.astype(F32)
    b = rest.astype(BF16)
    c = (rest - b.astype(F32)).astype(BF16)
    return a, b, c


def nt(a, b):
    return lax.dot_general(a, b, (((1,), (1,)), ((), ())), preferred_element_type=F32)


def dot(a, b):
    return jnp.dot(a, b, preferred_element_type=F32)


def body(
    samples, targets, index, centers, weights, nys, eig, coef, out_res, out_w,
    samp, targ, idx_v, idx_s, nys_v, eig_v, coef_v, wts, want,
    pts, cen, wlo, e123, ecat, psq, csq, kmat,
    part_p, part_m, rec1_p, rec1_m, red_p, red_m, rec2_p, rec2_m, rall, mall, gpart, grec, gs, gx,
    ld, zs, zr, ys, yr, xs, xr, cs, cr, s1, r1, s2, r2, gs1, gr1, gs2, gr2, ds, dr, dxs, dxr,
):
    blk, col = lax.axis_index("blk"), lax.axis_index("col")
    x, h, core = blk // 8, (blk // 2) % 4, blk % 2
    y, low = col // 2, col % 2
    z = 2 * h + low
    other = 1 - core

    def at_y(k):
        return spot(x, (y + k) % NY, z, core)

    def at_z(k):
        return spot(x, y, (z + k) % NZ, core)

    def at_x(k):
        return spot((x + k) % NX, y, z, core)

    partner = spot(x, y, z, other)

    def loop(n, fn, start=0):
        def run(k, carry):
            fn(k)
            return carry

        lax.fori_loop(start, n, run, 0)

    def peers(fn):
        loop(7, lambda i: fn(4 + (i + 1) // 2 * (1 - 2 * (i % 2))))

    barrier = pltpu.get_barrier_semaphore()

    def greet(where):
        pl.semaphore_signal(barrier, inc=1, device_id=where, device_id_type=MESH)

    peers(lambda k: greet(at_z(k)))
    peers(lambda k: greet(at_y(k)))
    for k in (2, 1, 3):
        greet(at_x(k))
    greet(partner)

    mine = 2 * x + core
    loads = [
        pltpu.make_async_copy(index, idx_v.at[0], ld.at[0]),
        pltpu.make_async_copy(samples, samp, ld.at[1]),
        pltpu.make_async_copy(centers, cen.at[mine], ld.at[2]),
        pltpu.make_async_copy(weights, wts, ld.at[3]),
        pltpu.make_async_copy(nys, nys_v.at[0], ld.at[4]),
        pltpu.make_async_copy(eig, eig_v, ld.at[5]),
        pltpu.make_async_copy(coef, coef_v.at[0], ld.at[6]),
        pltpu.make_async_copy(targets, targ, ld.at[7]),
        pltpu.make_async_copy(index, idx_s.at[0], ld.at[8]),
    ]
    for copy in loads:
        copy.start()
    for copy in loads[:2]:
        copy.wait()

    chosen = jnp.where(lax.broadcasted_iota(jnp.int32, (256, ROWS), 0) == idx_v[...], 1.0, 0.0).astype(F32)
    own = dot(chosen.T.astype(BF16), samp[...]).reshape(NY, 2, RUN, 768)
    own = jnp.concatenate([own[:, 0].reshape(64, 768), own[:, 1].reshape(64, 768)], axis=0)
    pts[h] = own.astype(BF16)

    pl.semaphore_wait(barrier, 18)
    if STAGE == 0:
        for copy in loads[2:]:
            copy.wait()
        return

    outward = 2 * low - 1
    zo, zi = spot(x, y, (z + outward + NZ) % NZ, core), spot(x, y, (z - outward + NZ) % NZ, core)
    h_a = ((z + outward + NZ) % NZ) // 2
    h_b = ((z - 2 * outward + NZ) % NZ) // 2
    h_c = ((z + 3 * outward + NZ) % NZ) // 2
    parity = y % 2
    y_to = (at_y(1), at_y(7))

    def zpiece(block, kind, i, where):
        piece = pts.at[block, pl.ds(pl.multiple_of(parity * 64 + i * 32, 32), 32), :]
        return send(piece, piece, (zs.at[kind, i], zr.at[kind, i]), where)

    def ypiece(block, kind, i, side):
        piece = pts.at[block, pl.ds(pl.multiple_of(side * 64 + i * 32, 32), 32), :]
        return send(piece, piece, (ys.at[kind, i], yr.at[kind, i]), y_to[i])

    x_next, x_prev, x_far = (x + 1) % NX, (x + 3) % NX, (x + 2) % NX
    right, left = at_x(1), at_x(3)

    def half(block_x, part_no, sem, where):
        piece = cen.at[2 * block_x + core, pl.ds(part_no * 64, 64), :]
        return send(piece, piece, (xs.at[sem], xr.at[sem]), where)

    def weight(block_x, sem, where):
        piece = wlo.at[2 * block_x + core]
        return send(piece, piece, (xs.at[sem], xr.at[sem]), where)

    def weight_half(block_x, part_no, sem, where):
        piece = wlo.at[2 * block_x + core, pl.ds(part_no * 64, 64), :]
        return send(piece, piece, (xs.at[sem], xr.at[sem]), where)

    def across(ref, block_core, block_x, sem):
        piece = ref.at[2 * block_x + block_core]
        return send(piece, piece, (cs.at[sem], cr.at[sem]), partner)

    for i in range(2):
        zpiece(h, 0, i, zo).start()
    loads[2].wait()
    half(x, 0, 0, right).start()
    half(x, 1, 1, left).start()
    half(x, 1, 2, right).start()
    half(x, 0, 3, left).start()
    across(cen, core, x, 0).start()

    for copy in loads[3:]:
        copy.wait()
    wlo[mine] = wts[...].astype(BF16)

    e1, e2, e3 = split3(eig_v[...])
    e123[:, 0:128] = e1
    e123[:, 128:256] = e2
    e123[:, 256:384] = e3

    def eig_rows(j):
        owner = ((j // 2) * 8 + h * 2 + j % 2) * 16 + col
        place = lax.broadcasted_iota(jnp.int32, (ROWS, 1536), 0) + owner * ROWS
        hit = jnp.where(place == nys_v[...], 1.0, 0.0).astype(BF16)
        ecat[j] = dot(hit, e123[...]).astype(BF16)

    def relay_a(i):
        zpiece(h_a, 0, i, zo).wait_recv()
        zpiece(h_a, 1, i, zi).start()
        ypiece(h_a, 0, i, parity).start()

    def relay_b(i):
        zpiece(h_b, 1, i, zi).wait_recv()
        zpiece(h_b, 2, i, zo).start()
        ypiece(h_b, 1, i, parity).start()

    def relay_c(i):
        zpiece(h_c, 2, i, zo).wait_recv()
        ypiece(h_c, 2, i, parity).start()

    def points_ready(t):
        p32 = pts[t].astype(F32)
        psq[t] = jnp.sum(p32 * p32, axis=1, keepdims=True)

    def from_y(block, kind):
        for i in range(2):
            ypiece(block, kind, i, 1 - parity).wait_recv()
        points_ready(block)

    def centers_ready(xp):
        for c in range(2):
            v = cen[2 * xp + c].astype(F32)
            total = jnp.sum(v * v, axis=1, keepdims=True)
            csq[xp, :, c * 128:(c + 1) * 128] = jnp.broadcast_to(total, (ROWS, ROWS)).T[0:8, :]

    def unit(t, xp):
        cross = nt(pts[t], cen[pl.ds(2 * xp, 2)].reshape(256, 768))
        dist = psq[t] + csq[xp, 0:1, :] - 2.0 * cross
        kmat[t, xp] = jnp.exp(-jnp.sqrt(dist + shift_sq)).astype(BF16)

    loop(4, eig_rows)
    relay_a(0)
    loop(6, eig_rows, 4)
    relay_a(1)
    half(x_prev, 0, 0, right).wait_recv()
    half(x_prev, 0, 4, right).start()
    half(x_next, 1, 1, left).wait_recv()
    half(x_next, 1, 5, left).start()
    loop(8, eig_rows, 6)
    relay_b(0)
    points_ready(h)
    across(cen, other, x, 0).wait_recv()
    centers_ready(x)
    relay_b(1)
    unit(h, x)
    half(x_prev, 1, 2, right).wait_recv()
    across(cen, core, x_prev, 1).start()
    half(x_next, 0, 3, left).wait_recv()
    across(cen, core, x_next, 2).start()
    weight(x, 6, right).start()
    weight(x, 7, left).start()
    across(wlo, core, x, 4).start()
    from_y(h_a, 0)
    unit(h_a, x)
    relay_c(0)
    across(cen, other, x_prev, 1).wait_recv()
    centers_ready(x_prev)
    across(cen, other, x_next, 2).wait_recv()
    centers_ready(x_next)
    unit(h, x_prev)
    unit(h, x_next)
    relay_c(1)
    half(x_far, 0, 4, right).wait_recv()
    half(x_far, 1, 5, left).wait_recv()
    across(cen, core, x_far, 3).start()
    weight(x_prev, 6, right).wait_recv()
    weight_half(x_prev, 0, 8, right).start()
    across(wlo, core, x_prev, 5).start()
    weight(x_next, 7, left).wait_recv()
    weight_half(x_next, 1, 9, left).start()
    across(wlo, core, x_next, 6).start()
    unit(h_a, x_prev)
    unit(h_a, x_next)
    from_y(h_b, 1)
    unit(h_b, x)
    unit(h_b, x_prev)
    unit(h_b, x_next)
    across(cen, other, x_far, 3).wait_recv()
    centers_ready(x_far)
    unit(h, x_far)
    unit(h_a, x_far)
    unit(h_b, x_far)
    weight_half(x_far, 0, 8, right).wait_recv()
    weight_half(x_far, 1, 9, left).wait_recv()
    across(wlo, core, x_far, 7).start()
    from_y(h_c, 2)
    unit(h_c, x)
    unit(h_c, x_prev)
    unit(h_c, x_next)
    unit(h_c, x_far)
    across(wlo, other, x, 4).wait_recv()
    across(wlo, other, x_prev, 5).wait_recv()
    across(wlo, other, x_next, 6).wait_recv()
    across(wlo, other, x_far, 7).wait_recv()

    def store(ref, by_z, t, value):
        if by_z:
            ref[pl.ds(2 * t, 2)] = value
        else:
            for i in range(2):
                ref[:, 2 * t + i] = value[i]

    def product(t):
        pred = jnp.zeros((ROWS, 256), F32)
        m = jnp.zeros((ROWS, 384), F32)
        for xp in range(NX):
            k = kmat[t, xp]
            pred += dot(k, wlo[2 * xp:2 * xp + 2].reshape(256, 256))
            m += dot(k, ecat[2 * xp:2 * xp + 2].reshape(256, 384))
        m = m[:, 0:128] + m[:, 128:256] + m[:, 256:384]
        pred, m = pred.reshape(2, 8, RUN, 256), m.reshape(2, 8, RUN, 128)

        @pl.when(core == 0)
        def _():
            store(part_p, False, t, pred)
            store(part_m, True, t, m)

        @pl.when(core == 1)
        def _():
            store(part_p, True, t, pred)
            store(part_m, False, t, m)

    loop(NH, product)

    pred_stream = (part_p, rec1_p, red_p, rec2_p, 0, core)
    m_stream = (part_m, rec1_m, red_m, rec2_m, 1, 1 - core)

    def axes(by_z):
        return y + by_z * (z - y), z + by_z * (y - z)

    def first(stream, k):
        part, rec1, _, _, no, by_z = stream
        where = spot(x, (y + (1 - by_z) * k) % NY, (z + by_z * k) % NZ, core)
        return send(part.at[(axes(by_z)[0] + k) % 8], rec1.at[k], (s1.at[no, k], r1.at[no, k]), where)

    def second(stream, k):
        _, _, red, rec2, no, by_z = stream
        where = spot(x, (y + by_z * k) % NY, (z + (1 - by_z) * k) % NZ, core)
        return send(red.at[(axes(by_z)[1] + k) % 8], rec2.at[k], (s2.at[no, k], r2.at[no, k]), where)

    def finish_first(stream):
        part, rec1, red, _, _, by_z = stream
        red[...] = part[axes(by_z)[0]]

        def add(k):
            first(stream, k).wait_recv()
            red[...] += rec1[k]

        loop(8, add, 1)
        peers(lambda k: second(stream, k).start())

    def finish_second(stream):
        _, _, red, rec2, _, by_z = stream

        def add(k, total):
            second(stream, k).wait_recv()
            return total + rec2[k]

        return lax.fori_loop(1, 8, add, red[axes(by_z)[1]])

    def r_first(k, src_y):
        return send(rall.at[z, src_y], rall.at[z, src_y], (gs1.at[0, k], gr1.at[0, k]), at_y(k))

    def r_second(k, src_z):
        return send(rall.at[src_z], rall.at[src_z], (gs2.at[0, k], gr2.at[0, k]), at_z(k))

    def m_first(k, src_z):
        return send(mall.at[src_z, y], mall.at[src_z, y], (gs1.at[1, k], gr1.at[1, k]), at_z(k))

    def m_second(k, src_y):
        return send(mall.at[:, src_y], mall.at[:, src_y], (gs2.at[1, k], gr2.at[1, k]), at_y(k))

    def swap(i):
        return send(gpart.at[i, other], grec.at[i], (ds.at[i], dr.at[i]), partner)

    def to_x(k):
        return send(gs.at[(x + k) % NX], gx.at[k], (dxs.at[k], dxr.at[k]), at_x(k))

    def drain(stage):
        if stage >= 1:
            for i in range(2):
                zpiece(h, 0, i, zo).wait_send()
                zpiece(h_a, 1, i, zi).wait_send()
                zpiece(h_b, 2, i, zo).wait_send()
                ypiece(h_a, 0, i, parity).wait_send()
                ypiece(h_b, 1, i, parity).wait_send()
                ypiece(h_c, 2, i, parity).wait_send()
            for i in range(6):
                half(x, 0, i, right).wait_send()
            for i in range(2):
                weight(x, 6 + i, right).wait_send()
                weight_half(x, 0, 8 + i, right).wait_send()
            for i in range(4):
                across(cen, core, x, i).wait_send()
                across(wlo, core, x, 4 + i).wait_send()
        if stage >= 3:
            for stream in (pred_stream, m_stream):
                loop(8, lambda k: first(stream, k).wait_send(), 1)
                loop(8, lambda k: second(stream, k).wait_send(), 1)
        if stage >= 4:
            loop(8, lambda k: r_first(k, y).wait_send(), 1)
            loop(8, lambda k: r_second(k, z).wait_send(), 1)
            loop(8, lambda k: m_first(k, z).wait_send(), 1)
            loop(8, lambda k: m_second(k, y).wait_send(), 1)
        if stage >= 5:
            for i in range(4):
                swap(i).wait_send()
            for k in (1, 2, 3):
                to_x(k).wait_send()

    if STAGE == 2:
        return drain(1)

    peers(lambda k: first(pred_stream, k).start())
    peers(lambda k: first(m_stream, k).start())
    for r in range(RUN):
        row = idx_s[0, col * RUN + r]
        want[r:r + 1, :] = targ[pl.ds(row, 1), :]
    finish_first(pred_stream)
    finish_first(m_stream)

    out_res[...] = finish_second(pred_stream) - want[...]
    rall[z, y] = out_res[...].astype(BF16)
    if STAGE == 3:
        finish_second(m_stream)
        return drain(3)

    peers(lambda k: r_first(k, y).start())
    mall[z, y] = finish_second(m_stream)
    peers(lambda k: m_first(k, z).start())
    loop(8, lambda k: r_first(k, (y - k + NY) % NY).wait_recv(), 1)
    peers(lambda k: r_second(k, z).start())
    loop(8, lambda k: m_first(k, (z - k + NZ) % NZ).wait_recv(), 1)
    peers(lambda k: m_second(k, y).start())
    loop(8, lambda k: r_second(k, (z - k + NZ) % NZ).wait_recv(), 1)
    loop(8, lambda k: m_second(k, (y - k + NY) % NY).wait_recv(), 1)
    if STAGE == 4:
        return drain(4)

    resid_t = rall[...].astype(F32).reshape(512, 256).T.astype(BF16)
    m1, m2, m3 = split3(mall[...].reshape(512, 128))
    proj = dot(resid_t, m1) + dot(resid_t, m2) + dot(resid_t, m3)
    a1, a2, a3 = split3(proj * coef_v[...])
    a_one = jnp.concatenate([a1, a1, a1], axis=1)
    a_two = jnp.concatenate([a2, a2], axis=1)

    def grad(xp):
        e = ecat[pl.ds(2 * xp, 2)].reshape(256, 384)
        g = dot(resid_t, kmat[:, xp].reshape(512, 256))
        g = g - (nt(a_one, e) + nt(a_two, e[:, 0:256]) + nt(a3, e[:, 0:128]))
        gpart[xp, 0] = g[:, 0:128]
        gpart[xp, 1] = g[:, 128:256]
        swap(xp).start()

    def summed(k):
        xp = (x + k) % NX
        swap(xp).wait_recv()
        gs[xp] = gpart[xp, core] + grec[xp]
        if k:
            to_x(k).start()

    grad(x_far)
    grad(x_next)
    summed(2)
    grad(x_prev)
    summed(1)
    grad(x)
    summed(3)
    summed(0)
    total = gs[x]
    for k in (1, 3, 2):
        to_x(k).wait_recv()
        total = total + gx[k]
    out_w[...] = wts[...] - step_size * total.T
    drain(5)


def local(samples, targets, batch_index, centers, weights, nystrom_index, eigvecs, coefficient):
    dma = pltpu.SemaphoreType.DMA
    vm = pltpu.VMEM
    return pl.pallas_call(
        body,
        out_shape=(jax.ShapeDtypeStruct((RUN, 256), F32), jax.ShapeDtypeStruct((ROWS, 256), F32)),
        in_specs=[pl.BlockSpec(memory_space=pl.ANY)] * 8,
        out_specs=(pl.BlockSpec(memory_space=pltpu.VMEM), pl.BlockSpec(memory_space=pltpu.VMEM)),
        scratch_shapes=[
            vm((256, 768), BF16), vm((256, 256), F32), vm((1, 128), jnp.int32), pltpu.SMEM((1, 128), jnp.int32),
            vm((1, 1536), jnp.int32), vm((1536, 128), F32), vm((1, 128), F32), vm((ROWS, 256), F32), vm((RUN, 256), F32),
            vm((NH, ROWS, 768), BF16), vm((8, ROWS, 768), BF16), vm((8, ROWS, 256), BF16),
            vm((1536, 384), BF16), vm((8, ROWS, 384), BF16),
            vm((NH, ROWS, 1), F32), vm((NX, 8, 256), F32), vm((NH, NX, ROWS, 256), BF16),
            vm((8, 8, RUN, 256), F32), vm((8, 8, RUN, 128), F32), vm((8, 8, RUN, 256), F32), vm((8, 8, RUN, 128), F32),
            vm((8, RUN, 256), F32), vm((8, RUN, 128), F32), vm((8, RUN, 256), F32), vm((8, RUN, 128), F32),
            vm((8, 8, RUN, 256), BF16), vm((8, 8, RUN, 128), F32),
            vm((NX, 2, 256, ROWS), F32), vm((NX, 256, ROWS), F32), vm((NX, 256, ROWS), F32), vm((NX, 256, ROWS), F32),
            dma((9,)), dma((3, 2)), dma((3, 2)), dma((3, 2)), dma((3, 2)), dma((10,)), dma((10,)), dma((8,)), dma((8,)),
            dma((2, 8)), dma((2, 8)), dma((2, 8)), dma((2, 8)),
            dma((2, 8)), dma((2, 8)), dma((2, 8)), dma((2, 8)), dma((4,)), dma((4,)), dma((4,)), dma((4,)),
        ],
        compiler_params=pltpu.CompilerParams(collective_id=0, has_side_effects=True, vmem_limit_bytes=67043328),
        name="step",
    )(samples, targets, batch_index, centers, weights, nystrom_index, eigvecs, coefficient)


def solution(mesh):
    in_specs = (
        P("blk", None),
        P("blk", None),
        P("blk"),
        P(("blk", "col"), None),
        P(("blk", "col"), None),
        P(),
        P(),
        P(),
    )
    out_specs = (P(("blk", "col"), None), P(("blk", "col"), None))
    return jax.shard_map(local, mesh=mesh, in_specs=in_specs, out_specs=out_specs, check_vma=False)
```

time: 880 us -> 77.1 us (0.09)
  waiting for transfers between devices: 652 us -> 0 us
  starting transfers between devices: 159 us -> 0 us
  Pallas kernels: 0 us -> 73.4 us
  matrix products: 21.7 us -> 0 us
  other arithmetic: 17.7 us -> 0 us
  between operations: 14.3 us -> 0.64 us
    ppermute x63 -> x0, waiting for transfers between devices: 288 us -> none  [shifted(): return lax.ppermute(block, axis, route)]
    psum x1 -> x0, waiting for transfers between devices: 262 us -> none  [local(): projected = lax.psum(local_proj, ('blk', 'col'))]
    ppermute x63 -> x0, starting transfers between devices: 148 us -> none  [shifted(): return lax.ppermute(block, axis, route)]
    pallas_call x0 -> x1, Pallas kernels: none -> 73.4 us  [local(): pl.pallas_call(body, out_shape=(jax.ShapeDtypeStruct((RUN, 256), F32), ja...]
    all_gather x1 -> x0, waiting for transfers between devices: 61.6 us -> none  [local(): lax.all_gather(residual_full.astype(jnp.bfloat16), 'blk', axis=0, tiled=T...]
    all_to_all x1 -> x0, waiting for transfers between devices: 41 us -> none  [copy_for_each(): lax.all_to_all(jnp.broadcast_to(x[None], (peers, *x.shape)), axis, 0, 0,...]
    dot_general x67 -> x0, matrix products: 21.7 us -> none  [the longest x32 8.24 us: kernel_block(): lax.dot_general(points, centers, (((1,), (1,)), ((), ())), preferred_elem...]
    all_to_all x1 -> x0, starting transfers between devices: 10.9 us -> none  [copy_for_each(): lax.all_to_all(jnp.broadcast_to(x[None], (peers, *x.shape)), axis, 0, 0,...]
  transfers between devices with their start and end apart: 66 -> 0, of which waited for: 35 -> 0; matrix products, arithmetic and copies ran while one was open for 2% -> 0% of each run, Pallas kernels for 0% -> 0%
where the time goes in v2:
time: 77.1 us; the launch traced here: 76.9 us
  Pallas kernels  73.4 us (95%)
  local copies, waits for them, and re-layouts  2.86 us (4%)
    pallas_call x1, Pallas kernels, local(): pl.pallas_call(body, out_shape=(jax.ShapeDtypeStruct((RUN, 256), F32), ja...  73.4 us
    unnamed x2, local copies, waits for them, and re-layouts  2.86 us

profile of v2, /device:TPU:1, one launch (start us, length us, event | category | flops | bytes accessed | tf_op | source)
XLA Modules:
  0.0 76.9 jit_solution(8429974562660538837)
XLA Ops:
  0.6 73.4 %step.1 = (f32[8,256]{1,0:T(8,128)}, f32[128,256]{1,0:T(8,128)}) custom-call(bf16[256,768]{1,0:T(8,128)(2,1)} %samples.1, f32[256,256]{1,0:T(8,128)} %targets.1, s32[128]{0:T(128)} %index.1, bf16[128,768]{1,0:T(8,128)(2,1)} %centers.1, f32[128,256]{1,0:T(8,128)} %weights.1, s32[1536]{0:T(1024)} %nys.1, f32[1536,128]{1,0:T(8,128)} %eig.1, f32[128]{0:T(128)} %coef.1), custom_call_target="tpu_custom_call" | custom-call | tf_op jit(solution)/shard_map/step/pallas_call | solution.py:462
  74.0 1.3 %copy.12 = f32[8,256]{1,0:T(8,128)} copy(f32[8,256]{1,0:T(8,128)} %get-tuple-element.4) | data formatting | bytes 16384
  75.3 1.6 %copy.13 = f32[128,256]{1,0:T(8,128)} copy(f32[128,256]{1,0:T(8,128)} %get-tuple-element.5) | data formatting | bytes 262144

commit v3 on v2

--- a/solution.py
+++ b/solution.py
@@ -48,7 +48,7 @@
     samp, targ, idx_v, idx_s, nys_v, eig_v, coef_v, wts, want,
     pts, cen, wlo, e123, ecat, psq, csq, kmat,
     part_p, part_m, rec1_p, rec1_m, red_p, red_m, rec2_p, rec2_m, rall, mall, gpart, grec, gs, gx,
-    ld, zs, zr, ys, yr, xs, xr, cs, cr, s1, r1, s2, r2, gs1, gr1, gs2, gr2, ds, dr, dxs, dxr,
+    ld, zs, zr, ys, yr, xs, xr, cs, cr, s1, r1, s2, r2, gs1, gr1, gs2, gr2, ds, dr, dxs, dxr, near,
 ):
     blk, col = lax.axis_index("blk"), lax.axis_index("col")
     x, h, core = blk // 8, (blk // 2) % 4, blk % 2
@@ -82,11 +82,8 @@
     def greet(where):
         pl.semaphore_signal(barrier, inc=1, device_id=where, device_id_type=MESH)
 
-    peers(lambda k: greet(at_z(k)))
-    peers(lambda k: greet(at_y(k)))
-    for k in (2, 1, 3):
-        greet(at_x(k))
-    greet(partner)
+    for where in (at_z(1), at_z(7), at_y(1), at_y(7), at_x(1), at_x(3), partner):
+        greet(where)
 
     mine = 2 * x + core
     loads = [
@@ -108,9 +105,9 @@
     chosen = jnp.where(lax.broadcasted_iota(jnp.int32, (256, ROWS), 0) == idx_v[...], 1.0, 0.0).astype(F32)
     own = dot(chosen.T.astype(BF16), samp[...]).reshape(NY, 2, RUN, 768)
     own = jnp.concatenate([own[:, 0].reshape(64, 768), own[:, 1].reshape(64, 768)], axis=0)
-    pts[h] = own.astype(BF16)
-
-    pl.semaphore_wait(barrier, 18)
+    pts[0] = own.astype(BF16)
+
+    pl.semaphore_wait(barrier, 7)
     if STAGE == 0:
         for copy in loads[2:]:
             copy.wait()
@@ -124,12 +121,12 @@
     parity = y % 2
     y_to = (at_y(1), at_y(7))
 
-    def zpiece(block, kind, i, where):
-        piece = pts.at[block, pl.ds(pl.multiple_of(parity * 64 + i * 32, 32), 32), :]
-        return send(piece, piece, (zs.at[kind, i], zr.at[kind, i]), where)
-
-    def ypiece(block, kind, i, side):
-        piece = pts.at[block, pl.ds(pl.multiple_of(side * 64 + i * 32, 32), 32), :]
+    def zpiece(kind, i, where):
+        rows = pl.ds(pl.multiple_of(parity * 64 + i * 32, 32), 32)
+        return send(pts.at[kind, rows, :], pts.at[kind + 1, rows, :], (zs.at[kind, i], zr.at[kind, i]), where)
+
+    def ypiece(kind, i, side):
+        piece = pts.at[kind + 1, pl.ds(pl.multiple_of(side * 64 + i * 32, 32), 32), :]
         return send(piece, piece, (ys.at[kind, i], yr.at[kind, i]), y_to[i])
 
     x_next, x_prev, x_far = (x + 1) % NX, (x + 3) % NX, (x + 2) % NX
@@ -151,8 +148,13 @@
         piece = ref.at[2 * block_x + block_core]
         return send(piece, piece, (cs.at[sem], cr.at[sem]), partner)
 
+    def hello(no, k):
+        for where in (at_y(k), at_y(8 - k)):
+            pl.semaphore_signal(near.at[no], inc=1, device_id=where, device_id_type=MESH)
+
     for i in range(2):
-        zpiece(h, 0, i, zo).start()
+        zpiece(0, i, zo).start()
+    hello(0, 1)
     loads[2].wait()
     half(x, 0, 0, right).start()
     half(x, 1, 1, left).start()
@@ -169,34 +171,34 @@
     e123[:, 128:256] = e2
     e123[:, 256:384] = e3
 
-    def eig_rows(j):
-        owner = ((j // 2) * 8 + h * 2 + j % 2) * 16 + col
+    def eig_rows(xp):
+        owner = (xp * 8 + h * 2 + core) * 16 + col
         place = lax.broadcasted_iota(jnp.int32, (ROWS, 1536), 0) + owner * ROWS
         hit = jnp.where(place == nys_v[...], 1.0, 0.0).astype(BF16)
-        ecat[j] = dot(hit, e123[...]).astype(BF16)
+        ecat[2 * xp + core] = dot(hit, e123[...]).astype(BF16)
 
     def relay_a(i):
-        zpiece(h_a, 0, i, zo).wait_recv()
-        zpiece(h_a, 1, i, zi).start()
-        ypiece(h_a, 0, i, parity).start()
+        zpiece(0, i, zo).wait_recv()
+        zpiece(1, i, zi).start()
+        ypiece(0, i, parity).start()
 
     def relay_b(i):
-        zpiece(h_b, 1, i, zi).wait_recv()
-        zpiece(h_b, 2, i, zo).start()
-        ypiece(h_b, 1, i, parity).start()
+        zpiece(1, i, zi).wait_recv()
+        zpiece(2, i, zo).start()
+        ypiece(1, i, parity).start()
 
     def relay_c(i):
-        zpiece(h_c, 2, i, zo).wait_recv()
-        ypiece(h_c, 2, i, parity).start()
-
-    def points_ready(t):
-        p32 = pts[t].astype(F32)
-        psq[t] = jnp.sum(p32 * p32, axis=1, keepdims=True)
-
-    def from_y(block, kind):
+        zpiece(2, i, zo).wait_recv()
+        ypiece(2, i, parity).start()
+
+    def points_ready(slot):
+        p32 = pts[slot].astype(F32)
+        psq[slot] = jnp.sum(p32 * p32, axis=1, keepdims=True)
+
+    def from_y(kind):
         for i in range(2):
-            ypiece(block, kind, i, 1 - parity).wait_recv()
-        points_ready(block)
+            ypiece(kind, i, 1 - parity).wait_recv()
+        points_ready(kind + 1)
 
     def centers_ready(xp):
         for c in range(2):
@@ -204,75 +206,75 @@
             total = jnp.sum(v * v, axis=1, keepdims=True)
             csq[xp, :, c * 128:(c + 1) * 128] = jnp.broadcast_to(total, (ROWS, ROWS)).T[0:8, :]
 
-    def unit(t, xp):
-        cross = nt(pts[t], cen[pl.ds(2 * xp, 2)].reshape(256, 768))
-        dist = psq[t] + csq[xp, 0:1, :] - 2.0 * cross
-        kmat[t, xp] = jnp.exp(-jnp.sqrt(dist + shift_sq)).astype(BF16)
-
-    loop(4, eig_rows)
+    def pair(xp):
+        return pl.ds(pl.multiple_of(xp * 256, 256), 256)
+
+    def unit(slot, end, xp):
+        rows = (end - slot) * ROWS
+        cross = nt(pts[slot:end].reshape(rows, 768), cen[pl.ds(2 * xp, 2)].reshape(256, 768))
+        shifted = psq[slot:end].reshape(rows, 1) + csq[xp, 0:1, :] - 2.0 * cross + shift_sq
+        kmat[slot * ROWS:end * ROWS, pair(xp)] = jnp.exp(-(shifted * lax.rsqrt(shifted))).astype(BF16)
+
+    loop(2, eig_rows)
     relay_a(0)
-    loop(6, eig_rows, 4)
+    pl.semaphore_wait(near.at[0], 2)
+    hello(1, 2)
+    loop(3, eig_rows, 2)
     relay_a(1)
     half(x_prev, 0, 0, right).wait_recv()
     half(x_prev, 0, 4, right).start()
     half(x_next, 1, 1, left).wait_recv()
     half(x_next, 1, 5, left).start()
-    loop(8, eig_rows, 6)
+    weight(x, 6, right).start()
+    weight(x, 7, left).start()
+    across(wlo, core, x, 4).start()
+    loop(4, eig_rows, 3)
+    for i in range(4):
+        across(ecat, core, i, 8 + i).start()
     relay_b(0)
-    points_ready(h)
+    points_ready(0)
     across(cen, other, x, 0).wait_recv()
     centers_ready(x)
     relay_b(1)
-    unit(h, x)
     half(x_prev, 1, 2, right).wait_recv()
     across(cen, core, x_prev, 1).start()
     half(x_next, 0, 3, left).wait_recv()
     across(cen, core, x_next, 2).start()
-    weight(x, 6, right).start()
-    weight(x, 7, left).start()
-    across(wlo, core, x, 4).start()
-    from_y(h_a, 0)
-    unit(h_a, x)
+    from_y(0)
+    unit(0, 2, x)
     relay_c(0)
     across(cen, other, x_prev, 1).wait_recv()
     centers_ready(x_prev)
     across(cen, other, x_next, 2).wait_recv()
     centers_ready(x_next)
-    unit(h, x_prev)
-    unit(h, x_next)
-    relay_c(1)
-    half(x_far, 0, 4, right).wait_recv()
-    half(x_far, 1, 5, left).wait_recv()
-    across(cen, core, x_far, 3).start()
+    unit(0, 2, x_prev)
     weight(x_prev, 6, right).wait_recv()
     weight_half(x_prev, 0, 8, right).start()
     across(wlo, core, x_prev, 5).start()
     weight(x_next, 7, left).wait_recv()
     weight_half(x_next, 1, 9, left).start()
     across(wlo, core, x_next, 6).start()
-    unit(h_a, x_prev)
-    unit(h_a, x_next)
-    from_y(h_b, 1)
-    unit(h_b, x)
-    unit(h_b, x_prev)
-    unit(h_b, x_next)
+    relay_c(1)
+    half(x_far, 0, 4, right).wait_recv()
+    half(x_far, 1, 5, left).wait_recv()
+    across(cen, core, x_far, 3).start()
+    unit(0, 2, x_next)
+    from_y(1)
     across(cen, other, x_far, 3).wait_recv()
     centers_ready(x_far)
-    unit(h, x_far)
-    unit(h_a, x_far)
-    unit(h_b, x_far)
+    unit(0, 3, x_far)
+    from_y(2)
+    unit(2, 4, x)
     weight_half(x_far, 0, 8, right).wait_recv()
     weight_half(x_far, 1, 9, left).wait_recv()
     across(wlo, core, x_far, 7).start()
-    from_y(h_c, 2)
-    unit(h_c, x)
-    unit(h_c, x_prev)
-    unit(h_c, x_next)
-    unit(h_c, x_far)
-    across(wlo, other, x, 4).wait_recv()
-    across(wlo, other, x_prev, 5).wait_recv()
-    across(wlo, other, x_next, 6).wait_recv()
-    across(wlo, other, x_far, 7).wait_recv()
+    unit(2, 4, x_prev)
+    unit(2, 4, x_next)
+    unit(3, 4, x_far)
+    for i, xp in enumerate((x, x_prev, x_next, x_far)):
+        across(wlo, other, xp, 4 + i).wait_recv()
+        across(ecat, other, i, 8 + i).wait_recv()
+    pl.semaphore_wait(near.at[1], 2)
 
     def store(ref, by_z, t, value):
         if by_z:
@@ -281,27 +283,22 @@
             for i in range(2):
                 ref[:, 2 * t + i] = value[i]
 
-    def product(t):
-        pred = jnp.zeros((ROWS, 256), F32)
-        m = jnp.zeros((ROWS, 384), F32)
-        for xp in range(NX):
-            k = kmat[t, xp]
-            pred += dot(k, wlo[2 * xp:2 * xp + 2].reshape(256, 256))
-            m += dot(k, ecat[2 * xp:2 * xp + 2].reshape(256, 384))
-        m = m[:, 0:128] + m[:, 128:256] + m[:, 256:384]
-        pred, m = pred.reshape(2, 8, RUN, 256), m.reshape(2, 8, RUN, 128)
-
-        @pl.when(core == 0)
-        def _():
-            store(part_p, False, t, pred)
-            store(part_m, True, t, m)
-
-        @pl.when(core == 1)
-        def _():
-            store(part_p, True, t, pred)
-            store(part_m, False, t, m)
-
-    loop(NH, product)
+    pred = dot(kmat[...], wlo[...].reshape(1024, 256)).reshape(NH, 2, 8, RUN, 256)
+    m = dot(kmat[...], ecat[...].reshape(1024, 384))
+    m = (m[:, 0:128] + m[:, 128:256] + m[:, 256:384]).reshape(NH, 2, 8, RUN, 128)
+    slots = (h, h_a, h_b, h_c)
+
+    @pl.when(core == 0)
+    def _():
+        for i in range(NH):
+            store(part_p, False, slots[i], pred[i])
+            store(part_m, True, slots[i], m[i])
+
+    @pl.when(core == 1)
+    def _():
+        for i in range(NH):
+            store(part_p, True, slots[i], pred[i])
+            store(part_m, False, slots[i], m[i])
 
     pred_stream = (part_p, rec1_p, red_p, rec2_p, 0, core)
     m_stream = (part_m, rec1_m, red_m, rec2_m, 1, 1 - core)
@@ -354,18 +351,30 @@
     def swap(i):
         return send(gpart.at[i, other], grec.at[i], (ds.at[i], dr.at[i]), partner)
 
-    def to_x(k):
-        return send(gs.at[(x + k) % NX], gx.at[k], (dxs.at[k], dxr.at[k]), at_x(k))
+    def top(ref):
+        return ref.at[0:128]
+
+    def bottom(ref):
+        return ref.at[128:256]
+
+    def far_half(i):
+        part_of = (top, bottom)[i]
+        return send(part_of(gs.at[x_far]), gx.at[2, pl.ds(128 * i, 128)], (dxs.at[i], dxr.at[i]), (right, left)[i])
+
+    def near_half(side, i):
+        part_of = (top, bottom)[i]
+        block, where = (gs.at[x_next], right) if side == 0 else (gs.at[x_prev], left)
+        sem = 2 + 2 * side + i
+        return send(part_of(block), gx.at[side, pl.ds(128 * i, 128)], (dxs.at[sem], dxr.at[sem]), where)
 
     def drain(stage):
         if stage >= 1:
             for i in range(2):
-                zpiece(h, 0, i, zo).wait_send()
-                zpiece(h_a, 1, i, zi).wait_send()
-                zpiece(h_b, 2, i, zo).wait_send()
-                ypiece(h_a, 0, i, parity).wait_send()
-                ypiece(h_b, 1, i, parity).wait_send()
-                ypiece(h_c, 2, i, parity).wait_send()
+                zpiece(0, i, zo).wait_send()
+                zpiece(1, i, zi).wait_send()
+                zpiece(2, i, zo).wait_send()
+                for kind in range(3):
+                    ypiece(kind, i, parity).wait_send()
             for i in range(6):
                 half(x, 0, i, right).wait_send()
             for i in range(2):
@@ -374,6 +383,7 @@
             for i in range(4):
                 across(cen, core, x, i).wait_send()
                 across(wlo, core, x, 4 + i).wait_send()
+                across(ecat, core, x, 8 + i).wait_send()
         if stage >= 3:
             for stream in (pred_stream, m_stream):
                 loop(8, lambda k: first(stream, k).wait_send(), 1)
@@ -386,8 +396,10 @@
         if stage >= 5:
             for i in range(4):
                 swap(i).wait_send()
-            for k in (1, 2, 3):
-                to_x(k).wait_send()
+            for i in range(2):
+                far_half(i).wait_send()
+                near_half(0, i).wait_send()
+                near_half(1, i).wait_send()
 
     if STAGE == 2:
         return drain(1)
@@ -418,8 +430,10 @@
     if STAGE == 4:
         return drain(4)
 
-    resid_t = rall[...].astype(F32).reshape(512, 256).T.astype(BF16)
-    m1, m2, m3 = split3(mall[...].reshape(512, 128))
+    resid = jnp.concatenate([rall[pl.ds(2 * t, 2)].astype(F32).reshape(ROWS, 256) for t in slots], axis=0)
+    resid_t = resid.T.astype(BF16)
+    m_slots = jnp.concatenate([mall[pl.ds(2 * t, 2)].reshape(ROWS, 128) for t in slots], axis=0)
+    m1, m2, m3 = split3(m_slots)
     proj = dot(resid_t, m1) + dot(resid_t, m2) + dot(resid_t, m3)
     a1, a2, a3 = split3(proj * coef_v[...])
     a_one = jnp.concatenate([a1, a1, a1], axis=1)
@@ -427,31 +441,39 @@
 
     def grad(xp):
         e = ecat[pl.ds(2 * xp, 2)].reshape(256, 384)
-        g = dot(resid_t, kmat[:, xp].reshape(512, 256))
+        g = dot(resid_t, kmat[:, pair(xp)])
         g = g - (nt(a_one, e) + nt(a_two, e[:, 0:256]) + nt(a3, e[:, 0:128]))
         gpart[xp, 0] = g[:, 0:128]
         gpart[xp, 1] = g[:, 128:256]
         swap(xp).start()
 
-    def summed(k):
-        xp = (x + k) % NX
+    def summed(xp):
         swap(xp).wait_recv()
         gs[xp] = gpart[xp, core] + grec[xp]
-        if k:
-            to_x(k).start()
 
     grad(x_far)
     grad(x_next)
-    summed(2)
+    summed(x_far)
+    far_half(0).start()
+    far_half(1).start()
     grad(x_prev)
-    summed(1)
+    summed(x_next)
+    near_half(0, 1).start()
     grad(x)
-    summed(3)
-    summed(0)
-    total = gs[x]
-    for k in (1, 3, 2):
-        to_x(k).wait_recv()
-        total = total + gx[k]
+    summed(x_prev)
+    near_half(1, 0).start()
+    far_half(0).wait_recv()
+    gs[x_next, 0:128, :] += gx[2, 0:128, :]
+    near_half(0, 0).start()
+    far_half(1).wait_recv()
+    gs[x_prev, 128:256, :] += gx[2, 128:256, :]
+    near_half(1, 1).start()
+    summed(x)
+    near_half(0, 1).wait_recv()
+    near_half(1, 0).wait_recv()
+    near_half(0, 0).wait_recv()
+    near_half(1, 1).wait_recv()
+    total = gs[x] + gx[0] + gx[1]
     out_w[...] = wts[...] - step_size * total.T
     drain(5)
 
@@ -469,14 +491,15 @@
             vm((1, 1536), jnp.int32), vm((1536, 128), F32), vm((1, 128), F32), vm((ROWS, 256), F32), vm((RUN, 256), F32),
             vm((NH, ROWS, 768), BF16), vm((8, ROWS, 768), BF16), vm((8, ROWS, 256), BF16),
             vm((1536, 384), BF16), vm((8, ROWS, 384), BF16),
-            vm((NH, ROWS, 1), F32), vm((NX, 8, 256), F32), vm((NH, NX, ROWS, 256), BF16),
+            vm((NH, ROWS, 1), F32), vm((NX, 8, 256), F32), vm((NH * ROWS, 1024), BF16),
             vm((8, 8, RUN, 256), F32), vm((8, 8, RUN, 128), F32), vm((8, 8, RUN, 256), F32), vm((8, 8, RUN, 128), F32),
             vm((8, RUN, 256), F32), vm((8, RUN, 128), F32), vm((8, RUN, 256), F32), vm((8, RUN, 128), F32),
             vm((8, 8, RUN, 256), BF16), vm((8, 8, RUN, 128), F32),
-            vm((NX, 2, 256, ROWS), F32), vm((NX, 256, ROWS), F32), vm((NX, 256, ROWS), F32), vm((NX, 256, ROWS), F32),
-            dma((9,)), dma((3, 2)), dma((3, 2)), dma((3, 2)), dma((3, 2)), dma((10,)), dma((10,)), dma((8,)), dma((8,)),
+            vm((NX, 2, 256, ROWS), F32), vm((NX, 256, ROWS), F32), vm((NX, 256, ROWS), F32), vm((3, 256, ROWS), F32),
+            dma((9,)), dma((3, 2)), dma((3, 2)), dma((3, 2)), dma((3, 2)), dma((10,)), dma((10,)), dma((12,)), dma((12,)),
             dma((2, 8)), dma((2, 8)), dma((2, 8)), dma((2, 8)),
-            dma((2, 8)), dma((2, 8)), dma((2, 8)), dma((2, 8)), dma((4,)), dma((4,)), dma((4,)), dma((4,)),
+            dma((2, 8)), dma((2, 8)), dma((2, 8)), dma((2, 8)), dma((4,)), dma((4,)), dma((6,)), dma((6,)),
+            pltpu.SemaphoreType.REGULAR((2,)),
         ],
         compiler_params=pltpu.CompilerParams(collective_id=0, has_side_effects=True, vmem_limit_bytes=67043328),
         name="step",

time: 77.1 us -> 73.8 us (0.957)
  Pallas kernels: 73.4 us -> 70.1 us
    pallas_call x1, Pallas kernels: 73.4 us -> 70.1 us  [local(): pl.pallas_call(body, out_shape=(jax.ShapeDtypeStruct((RUN, 256), F32), ja...]
where the time goes in v3:
time: 73.8 us; the launch traced here: 73.6 us
  Pallas kernels  70.1 us (95%)
  local copies, waits for them, and re-layouts  2.86 us (4%)
    pallas_call x1, Pallas kernels, local(): pl.pallas_call(body, out_shape=(jax.ShapeDtypeStruct((RUN, 256), F32), ja...  70.1 us
    unnamed x2, local copies, waits for them, and re-layouts  2.86 us

profile of v3, /device:TPU:1, one launch (start us, length us, event | category | flops | bytes accessed | tf_op | source)
XLA Modules:
  0.0 73.6 jit_solution(7693149417119269284)
XLA Ops:
  0.6 70.1 %step.1 = (f32[8,256]{1,0:T(8,128)}, f32[128,256]{1,0:T(8,128)}) custom-call(bf16[256,768]{1,0:T(8,128)(2,1)} %samples.1, f32[256,256]{1,0:T(8,128)} %targets.1, s32[128]{0:T(128)} %index.1, bf16[128,768]{1,0:T(8,128)(2,1)} %centers.1, f32[128,256]{1,0:T(8,128)} %weights.1, s32[1536]{0:T(1024)} %nys.1, f32[1536,128]{1,0:T(8,128)} %eig.1, f32[128]{0:T(128)} %coef.1), custom_call_target="tpu_custom_call" | custom-call | tf_op jit(solution)/shard_map/step/pallas_call | solution.py:484
  70.8 1.3 %copy.12 = f32[8,256]{1,0:T(8,128)} copy(f32[8,256]{1,0:T(8,128)} %get-tuple-element.4) | data formatting | bytes 16384
  72.1 1.6 %copy.13 = f32[128,256]{1,0:T(8,128)} copy(f32[128,256]{1,0:T(8,128)} %get-tuple-element.5) | data formatting | bytes 262144

commit v4 on v3

--- a/solution.py
+++ b/solution.py
@@ -44,12 +44,13 @@
 
 
 def body(
-    samples, targets, index, centers, weights, nys, eig, coef, out_res, out_w,
+    samples, targets, index, centers, weights, nys, eig, coef, out,
     samp, targ, idx_v, idx_s, nys_v, eig_v, coef_v, wts, want,
     pts, cen, wlo, e123, ecat, psq, csq, kmat,
-    part_p, part_m, rec1_p, rec1_m, red_p, red_m, rec2_p, rec2_m, rall, mall, gpart, grec, gs, gx,
-    ld, zs, zr, ys, yr, xs, xr, cs, cr, s1, r1, s2, r2, gs1, gr1, gs2, gr2, ds, dr, dxs, dxr, near,
+    part_py, rec_py, part_pz, rec_pz, part_my, rec_my, part_mz, rec_mz, red_p, red_m, rec2_p, rec2_m, rall, mall, gpart, grec, gs, gx,
+    ld, zs, zr, ys, yr, xs, xr, cs, cr, sy, ry, sz, rz, s2, r2, gs1, gr1, gs2, gr2, ds, dr, dxs, dxr, near,
 ):
+    out_res, out_w = out.at[0:RUN], out.at[RUN:RUN + ROWS]
     blk, col = lax.axis_index("blk"), lax.axis_index("col")
     x, h, core = blk // 8, (blk // 2) % 4, blk % 2
     y, low = col // 2, col % 2
@@ -107,9 +108,12 @@
     own = jnp.concatenate([own[:, 0].reshape(64, 768), own[:, 1].reshape(64, 768)], axis=0)
     pts[0] = own.astype(BF16)
 
+    loads[3].wait()
+    wlo[mine] = wts[...].astype(BF16)
+
     pl.semaphore_wait(barrier, 7)
     if STAGE == 0:
-        for copy in loads[2:]:
+        for copy in (loads[2], *loads[4:]):
             copy.wait()
         return
 
@@ -161,10 +165,12 @@
     half(x, 1, 2, right).start()
     half(x, 0, 3, left).start()
     across(cen, core, x, 0).start()
-
-    for copy in loads[3:]:
+    weight(x, 6, right).start()
+    weight(x, 7, left).start()
+    across(wlo, core, x, 4).start()
+
+    for copy in loads[4:]:
         copy.wait()
-    wlo[mine] = wts[...].astype(BF16)
 
     e1, e2, e3 = split3(eig_v[...])
     e123[:, 0:128] = e1
@@ -215,22 +221,17 @@
         shifted = psq[slot:end].reshape(rows, 1) + csq[xp, 0:1, :] - 2.0 * cross + shift_sq
         kmat[slot * ROWS:end * ROWS, pair(xp)] = jnp.exp(-(shifted * lax.rsqrt(shifted))).astype(BF16)
 
-    loop(2, eig_rows)
+    loop(4, eig_rows)
+    for i in range(4):
+        across(ecat, core, i, 8 + i).start()
     relay_a(0)
     pl.semaphore_wait(near.at[0], 2)
     hello(1, 2)
-    loop(3, eig_rows, 2)
     relay_a(1)
     half(x_prev, 0, 0, right).wait_recv()
     half(x_prev, 0, 4, right).start()
     half(x_next, 1, 1, left).wait_recv()
     half(x_next, 1, 5, left).start()
-    weight(x, 6, right).start()
-    weight(x, 7, left).start()
-    across(wlo, core, x, 4).start()
-    loop(4, eig_rows, 3)
-    for i in range(4):
-        across(ecat, core, i, 8 + i).start()
     relay_b(0)
     points_ready(0)
     across(cen, other, x, 0).wait_recv()
@@ -240,101 +241,145 @@
     across(cen, core, x_prev, 1).start()
     half(x_next, 0, 3, left).wait_recv()
     across(cen, core, x_next, 2).start()
-    from_y(0)
-    unit(0, 2, x)
-    relay_c(0)
-    across(cen, other, x_prev, 1).wait_recv()
-    centers_ready(x_prev)
-    across(cen, other, x_next, 2).wait_recv()
-    centers_ready(x_next)
-    unit(0, 2, x_prev)
     weight(x_prev, 6, right).wait_recv()
     weight_half(x_prev, 0, 8, right).start()
     across(wlo, core, x_prev, 5).start()
     weight(x_next, 7, left).wait_recv()
     weight_half(x_next, 1, 9, left).start()
     across(wlo, core, x_next, 6).start()
-    relay_c(1)
+    from_y(0)
+    unit(0, 2, x)
+    relay_c(0)
     half(x_far, 0, 4, right).wait_recv()
     half(x_far, 1, 5, left).wait_recv()
     across(cen, core, x_far, 3).start()
+    across(cen, other, x_prev, 1).wait_recv()
+    centers_ready(x_prev)
+    across(cen, other, x_next, 2).wait_recv()
+    centers_ready(x_next)
+    unit(0, 2, x_prev)
+    relay_c(1)
+    weight_half(x_far, 0, 8, right).wait_recv()
+    weight_half(x_far, 1, 9, left).wait_recv()
+    across(wlo, core, x_far, 7).start()
     unit(0, 2, x_next)
     from_y(1)
     across(cen, other, x_far, 3).wait_recv()
     centers_ready(x_far)
-    unit(0, 3, x_far)
-    from_y(2)
-    unit(2, 4, x)
-    weight_half(x_far, 0, 8, right).wait_recv()
-    weight_half(x_far, 1, 9, left).wait_recv()
-    across(wlo, core, x_far, 7).start()
-    unit(2, 4, x_prev)
-    unit(2, 4, x_next)
-    unit(3, 4, x_far)
+    unit(0, 2, x_far)
     for i, xp in enumerate((x, x_prev, x_next, x_far)):
         across(wlo, other, xp, 4 + i).wait_recv()
         across(ecat, other, i, 8 + i).wait_recv()
     pl.semaphore_wait(near.at[1], 2)
 
-    def store(ref, by_z, t, value):
-        if by_z:
-            ref[pl.ds(2 * t, 2)] = value
+    slots = (h, h_a, h_b, h_c)
+    pred_stream = (part_py, rec_py, part_pz, rec_pz, red_p, rec2_p, 0)
+    m_stream = (part_my, rec_my, part_mz, rec_mz, red_m, rec2_m, 1)
+
+    def y_first(stream, g, k):
+        no = stream[6]
+        return send(stream[0].at[g, (y + k) % NY], stream[1].at[g, k], (sy.at[no, g, k], ry.at[no, g, k]), at_y(k))
+
+    def z_first(stream, k):
+        no = stream[6]
+        return send(stream[2].at[(z + k) % NZ], stream[3].at[k], (sz.at[no, k], rz.at[no, k]), at_z(k))
+
+    def launch_y(stream, g, value):
+        for i in range(2):
+            for j in range(2):
+                stream[0][g, :, 2 * i + j] = value[i, j]
+        peers(lambda k: y_first(stream, g, k).start())
+
+    def launch_z(stream, g, value):
+        for i in range(2):
+            stream[2][pl.ds(2 * slots[2 * g + i], 2)] = value[i]
+        targets = []
+        if g == 0:
+            targets.append(2 * h + 1 - low)
         else:
-            for i in range(2):
-                ref[:, 2 * t + i] = value[i]
-
-    pred = dot(kmat[...], wlo[...].reshape(1024, 256)).reshape(NH, 2, 8, RUN, 256)
-    m = dot(kmat[...], ecat[...].reshape(1024, 384))
-    m = (m[:, 0:128] + m[:, 128:256] + m[:, 256:384]).reshape(NH, 2, 8, RUN, 128)
-    slots = (h, h_a, h_b, h_c)
-
-    @pl.when(core == 0)
-    def _():
-        for i in range(NH):
-            store(part_p, False, slots[i], pred[i])
-            store(part_m, True, slots[i], m[i])
-
-    @pl.when(core == 1)
-    def _():
-        for i in range(NH):
-            store(part_p, True, slots[i], pred[i])
-            store(part_m, False, slots[i], m[i])
-
-    pred_stream = (part_p, rec1_p, red_p, rec2_p, 0, core)
-    m_stream = (part_m, rec1_m, red_m, rec2_m, 1, 1 - core)
+            targets += [2 * h_c, 2 * h_c + 1]
+        between = h_a if g == 0 else h_b
+        targets += [2 * between, 2 * between + 1]
+        for target in targets:
+            z_first(stream, (target - z + NZ) % NZ).start()
+
+    def group(g):
+        k = kmat[256 * g:256 * g + 256, :]
+        pred = dot(k, wlo[...].reshape(1024, 256)).reshape(2, 2, 8, RUN, 256)
+        m = dot(k, ecat[...].reshape(1024, 384))
+        m = (m[:, 0:128] + m[:, 128:256] + m[:, 256:384]).reshape(2, 2, 8, RUN, 128)
+
+        @pl.when(core == 0)
+        def _():
+            launch_y(pred_stream, g, pred)
+            launch_z(m_stream, g, m)
+
+        @pl.when(core == 1)
+        def _():
+            launch_z(pred_stream, g, pred)
+            launch_y(m_stream, g, m)
+
+    group(0)
+    from_y(2)
+    unit(2, 4, x)
+    unit(2, 4, x_prev)
+    unit(2, 4, x_next)
+    unit(2, 4, x_far)
+    group(1)
 
     def axes(by_z):
         return y + by_z * (z - y), z + by_z * (y - z)
 
-    def first(stream, k):
-        part, rec1, _, _, no, by_z = stream
-        where = spot(x, (y + (1 - by_z) * k) % NY, (z + by_z * k) % NZ, core)
-        return send(part.at[(axes(by_z)[0] + k) % 8], rec1.at[k], (s1.at[no, k], r1.at[no, k]), where)
+    def by_z(stream):
+        return core if stream[6] == 0 else 1 - core
 
     def second(stream, k):
-        _, _, red, rec2, no, by_z = stream
-        where = spot(x, (y + by_z * k) % NY, (z + (1 - by_z) * k) % NZ, core)
-        return send(red.at[(axes(by_z)[1] + k) % 8], rec2.at[k], (s2.at[no, k], r2.at[no, k]), where)
+        flag = by_z(stream)
+        no = stream[6]
+        where = spot(x, (y + flag * k) % NY, (z + (1 - flag) * k) % NZ, core)
+        return send(stream[4].at[(axes(flag)[1] + k) % 8], stream[5].at[k], (s2.at[no, k], r2.at[no, k]), where)
 
     def finish_first(stream):
-        part, rec1, red, _, _, by_z = stream
-        red[...] = part[axes(by_z)[0]]
-
-        def add(k):
-            first(stream, k).wait_recv()
-            red[...] += rec1[k]
-
-        loop(8, add, 1)
+        @pl.when(by_z(stream) == 0)
+        def _():
+            for g in range(2):
+
+                def add(k, total):
+                    y_first(stream, g, k).wait_recv()
+                    return total + stream[1][g, k]
+
+                total = lax.fori_loop(1, 8, add, stream[0][g, y])
+                for i in range(2):
+                    stream[4][pl.ds(2 * slots[2 * g + i], 2)] = total[2 * i:2 * i + 2]
+
+        @pl.when(by_z(stream) == 1)
+        def _():
+            stream[4][...] = stream[2][z]
+
+            def add(k):
+                z_first(stream, k).wait_recv()
+                stream[4][...] += stream[3][k]
+
+            loop(8, add, 1)
+
         peers(lambda k: second(stream, k).start())
 
+    def sent_first(stream):
+        @pl.when(by_z(stream) == 0)
+        def _():
+            for g in range(2):
+                loop(8, lambda k: y_first(stream, g, k).wait_send(), 1)
+
+        @pl.when(by_z(stream) == 1)
+        def _():
+            loop(8, lambda k: z_first(stream, k).wait_send(), 1)
+
     def finish_second(stream):
-        _, _, red, rec2, _, by_z = stream
-
         def add(k, total):
             second(stream, k).wait_recv()
-            return total + rec2[k]
-
-        return lax.fori_loop(1, 8, add, red[axes(by_z)[1]])
+            return total + stream[5][k]
+
+        return lax.fori_loop(1, 8, add, stream[4][axes(by_z(stream))[1]])
 
     def r_first(k, src_y):
         return send(rall.at[z, src_y], rall.at[z, src_y], (gs1.at[0, k], gr1.at[0, k]), at_y(k))
@@ -386,7 +431,7 @@
                 across(ecat, core, x, 8 + i).wait_send()
         if stage >= 3:
             for stream in (pred_stream, m_stream):
-                loop(8, lambda k: first(stream, k).wait_send(), 1)
+                sent_first(stream)
                 loop(8, lambda k: second(stream, k).wait_send(), 1)
         if stage >= 4:
             loop(8, lambda k: r_first(k, y).wait_send(), 1)
@@ -401,11 +446,6 @@
                 near_half(0, i).wait_send()
                 near_half(1, i).wait_send()
 
-    if STAGE == 2:
-        return drain(1)
-
-    peers(lambda k: first(pred_stream, k).start())
-    peers(lambda k: first(m_stream, k).start())
     for r in range(RUN):
         row = idx_s[0, col * RUN + r]
         want[r:r + 1, :] = targ[pl.ds(row, 1), :]
@@ -481,29 +521,31 @@
 def local(samples, targets, batch_index, centers, weights, nystrom_index, eigvecs, coefficient):
     dma = pltpu.SemaphoreType.DMA
     vm = pltpu.VMEM
-    return pl.pallas_call(
+    out = pl.pallas_call(
         body,
-        out_shape=(jax.ShapeDtypeStruct((RUN, 256), F32), jax.ShapeDtypeStruct((ROWS, 256), F32)),
+        out_shape=jax.ShapeDtypeStruct((RUN + ROWS, 256), F32),
         in_specs=[pl.BlockSpec(memory_space=pl.ANY)] * 8,
-        out_specs=(pl.BlockSpec(memory_space=pltpu.VMEM), pl.BlockSpec(memory_space=pltpu.VMEM)),
+        out_specs=pl.BlockSpec(memory_space=pltpu.VMEM),
         scratch_shapes=[
             vm((256, 768), BF16), vm((256, 256), F32), vm((1, 128), jnp.int32), pltpu.SMEM((1, 128), jnp.int32),
             vm((1, 1536), jnp.int32), vm((1536, 128), F32), vm((1, 128), F32), vm((ROWS, 256), F32), vm((RUN, 256), F32),
             vm((NH, ROWS, 768), BF16), vm((8, ROWS, 768), BF16), vm((8, ROWS, 256), BF16),
             vm((1536, 384), BF16), vm((8, ROWS, 384), BF16),
             vm((NH, ROWS, 1), F32), vm((NX, 8, 256), F32), vm((NH * ROWS, 1024), BF16),
-            vm((8, 8, RUN, 256), F32), vm((8, 8, RUN, 128), F32), vm((8, 8, RUN, 256), F32), vm((8, 8, RUN, 128), F32),
+            vm((2, 8, 4, RUN, 256), F32), vm((2, 8, 4, RUN, 256), F32), vm((8, 8, RUN, 256), F32), vm((8, 8, RUN, 256), F32),
+            vm((2, 8, 4, RUN, 128), F32), vm((2, 8, 4, RUN, 128), F32), vm((8, 8, RUN, 128), F32), vm((8, 8, RUN, 128), F32),
             vm((8, RUN, 256), F32), vm((8, RUN, 128), F32), vm((8, RUN, 256), F32), vm((8, RUN, 128), F32),
             vm((8, 8, RUN, 256), BF16), vm((8, 8, RUN, 128), F32),
             vm((NX, 2, 256, ROWS), F32), vm((NX, 256, ROWS), F32), vm((NX, 256, ROWS), F32), vm((3, 256, ROWS), F32),
             dma((9,)), dma((3, 2)), dma((3, 2)), dma((3, 2)), dma((3, 2)), dma((10,)), dma((10,)), dma((12,)), dma((12,)),
-            dma((2, 8)), dma((2, 8)), dma((2, 8)), dma((2, 8)),
+            dma((2, 2, 8)), dma((2, 2, 8)), dma((2, 8)), dma((2, 8)), dma((2, 8)), dma((2, 8)),
             dma((2, 8)), dma((2, 8)), dma((2, 8)), dma((2, 8)), dma((4,)), dma((4,)), dma((6,)), dma((6,)),
             pltpu.SemaphoreType.REGULAR((2,)),
         ],
         compiler_params=pltpu.CompilerParams(collective_id=0, has_side_effects=True, vmem_limit_bytes=67043328),
         name="step",
     )(samples, targets, batch_index, centers, weights, nystrom_index, eigvecs, coefficient)
+    return out[0:RUN], out[RUN:]
 
 
 def solution(mesh):

time: 73.8 us -> 72 us (0.976)
  Pallas kernels: 70.1 us -> 68.3 us
    slice x0 -> x2, local copies, waits for them, and re-layouts: none -> 2.86 us  [local(): return (out[0:RUN], out[RUN:])]
    unnamed x2 -> x0, local copies, waits for them, and re-layouts: 2.86 us -> none
    pallas_call x1, Pallas kernels: 70.1 us -> 68.3 us  [local(): pl.pallas_call(body, out_shape=jax.ShapeDtypeStruct((RUN + ROWS, 256), F3...]
where the time goes in v4:
time: 72 us; the launch traced here: 71.8 us
  Pallas kernels  68.3 us (95%)
  local copies, waits for them, and re-layouts  2.86 us (4%)
    pallas_call x1, Pallas kernels, local(): pl.pallas_call(body, out_shape=jax.ShapeDtypeStruct((RUN + ROWS, 256), F3...  68.3 us
    slice x2, local copies, waits for them, and re-layouts, local(): return (out[0:RUN], out[RUN:])  2.86 us

profile of v4, /device:TPU:1, one launch (start us, length us, event | category | flops | bytes accessed | tf_op | source)
XLA Modules:
  0.0 71.8 jit_solution(18076867583031066076)
XLA Ops:
  0.6 68.3 %step.1 = f32[136,256]{1,0:T(8,128)} custom-call(bf16[256,768]{1,0:T(8,128)(2,1)} %samples.1, f32[256,256]{1,0:T(8,128)} %targets.1, s32[128]{0:T(128)} %index.1, bf16[128,768]{1,0:T(8,128)(2,1)} %centers.1, f32[128,256]{1,0:T(8,128)} %weights.1, s32[1536]{0:T(1024)} %nys.1, f32[1536,128]{1,0:T(8,128)} %eig.1, f32[128]{0:T(128)} %coef.1), custom_call_target="tpu_custom_call" | custom-call | tf_op jit(solution)/shard_map/step/pallas_call | solution.py:524
  69.0 1.3 %slice.6 = f32[8,256]{1,0:T(8,128)} slice(f32[136,256]{1,0:T(8,128)} %step.1), slice={[0:8], [0:256]} | slice | bytes 16384 | tf_op jit(solution)/shard_map/slice | solution.py:548
  70.3 1.6 %slice.7 = f32[128,256]{1,0:T(8,128)} slice(f32[136,256]{1,0:T(8,128)} %step.1), slice={[8:136], [0:256]} | slice | bytes 262144 | tf_op jit(solution)/shard_map/slice | solution.py:548

commit v5 on v4

--- a/solution.py
+++ b/solution.py
@@ -106,7 +106,7 @@
     chosen = jnp.where(lax.broadcasted_iota(jnp.int32, (256, ROWS), 0) == idx_v[...], 1.0, 0.0).astype(F32)
     own = dot(chosen.T.astype(BF16), samp[...]).reshape(NY, 2, RUN, 768)
     own = jnp.concatenate([own[:, 0].reshape(64, 768), own[:, 1].reshape(64, 768)], axis=0)
-    pts[0] = own.astype(BF16)
+    pts[2] = own.astype(BF16)
 
     loads[3].wait()
     wlo[mine] = wts[...].astype(BF16)
@@ -125,12 +125,14 @@
     parity = y % 2
     y_to = (at_y(1), at_y(7))
 
+    held_in, lands_in = (2, 0, 1), (0, 1, 3)
+
     def zpiece(kind, i, where):
         rows = pl.ds(pl.multiple_of(parity * 64 + i * 32, 32), 32)
-        return send(pts.at[kind, rows, :], pts.at[kind + 1, rows, :], (zs.at[kind, i], zr.at[kind, i]), where)
+        return send(pts.at[held_in[kind], rows, :], pts.at[lands_in[kind], rows, :], (zs.at[kind, i], zr.at[kind, i]), where)
 
     def ypiece(kind, i, side):
-        piece = pts.at[kind + 1, pl.ds(pl.multiple_of(side * 64 + i * 32, 32), 32), :]
+        piece = pts.at[lands_in[kind], pl.ds(pl.multiple_of(side * 64 + i * 32, 32), 32), :]
         return send(piece, piece, (ys.at[kind, i], yr.at[kind, i]), y_to[i])
 
     x_next, x_prev, x_far = (x + 1) % NX, (x + 3) % NX, (x + 2) % NX
@@ -204,7 +206,7 @@
     def from_y(kind):
         for i in range(2):
             ypiece(kind, i, 1 - parity).wait_recv()
-        points_ready(kind + 1)
+        points_ready(lands_in[kind])
 
     def centers_ready(xp):
         for c in range(2):
@@ -233,7 +235,7 @@
     half(x_next, 1, 1, left).wait_recv()
     half(x_next, 1, 5, left).start()
     relay_b(0)
-    points_ready(0)
+    points_ready(2)
     across(cen, other, x, 0).wait_recv()
     centers_ready(x)
     relay_b(1)
@@ -248,22 +250,22 @@
     weight_half(x_next, 1, 9, left).start()
     across(wlo, core, x_next, 6).start()
     from_y(0)
-    unit(0, 2, x)
-    relay_c(0)
     half(x_far, 0, 4, right).wait_recv()
     half(x_far, 1, 5, left).wait_recv()
     across(cen, core, x_far, 3).start()
+    relay_c(0)
     across(cen, other, x_prev, 1).wait_recv()
     centers_ready(x_prev)
     across(cen, other, x_next, 2).wait_recv()
     centers_ready(x_next)
-    unit(0, 2, x_prev)
     relay_c(1)
+    from_y(1)
+    unit(0, 2, x)
     weight_half(x_far, 0, 8, right).wait_recv()
     weight_half(x_far, 1, 9, left).wait_recv()
     across(wlo, core, x_far, 7).start()
+    unit(0, 2, x_prev)
     unit(0, 2, x_next)
-    from_y(1)
     across(cen, other, x_far, 3).wait_recv()
     centers_ready(x_far)
     unit(0, 2, x_far)
@@ -272,7 +274,7 @@
         across(ecat, other, i, 8 + i).wait_recv()
     pl.semaphore_wait(near.at[1], 2)
 
-    slots = (h, h_a, h_b, h_c)
+    slots = (h_a, h_b, h, h_c)
     pred_stream = (part_py, rec_py, part_pz, rec_pz, red_p, rec2_p, 0)
     m_stream = (part_my, rec_my, part_mz, rec_mz, red_m, rec2_m, 1)
 
@@ -293,13 +295,10 @@
     def launch_z(stream, g, value):
         for i in range(2):
             stream[2][pl.ds(2 * slots[2 * g + i], 2)] = value[i]
-        targets = []
         if g == 0:
-            targets.append(2 * h + 1 - low)
+            targets = (2 * h_b, 2 * h_b + 1, 2 * h_a, 2 * h_a + 1)
         else:
-            targets += [2 * h_c, 2 * h_c + 1]
-        between = h_a if g == 0 else h_b
-        targets += [2 * between, 2 * between + 1]
+            targets = (2 * h_c, 2 * h_c + 1, 2 * h + 1 - low)
         for target in targets:
             z_first(stream, (target - z + NZ) % NZ).start()
 
@@ -492,10 +491,10 @@
         gs[xp] = gpart[xp, core] + grec[xp]
 
     grad(x_far)
-    grad(x_next)
     summed(x_far)
     far_half(0).start()
     far_half(1).start()
+    grad(x_next)
     grad(x_prev)
     summed(x_next)
     near_half(0, 1).start()

time: 72 us -> 70.5 us (0.979)
  Pallas kernels: 68.3 us -> 66.8 us
    pallas_call x1, Pallas kernels: 68.3 us -> 66.8 us  [local(): pl.pallas_call(body, out_shape=jax.ShapeDtypeStruct((RUN + ROWS, 256), F3...]
where the time goes in v5:
time: 70.5 us; the launch traced here: 70.3 us
  Pallas kernels  66.8 us (95%)
  local copies, waits for them, and re-layouts  2.86 us (4%)
    pallas_call x1, Pallas kernels, local(): pl.pallas_call(body, out_shape=jax.ShapeDtypeStruct((RUN + ROWS, 256), F3...  66.8 us
    slice x2, local copies, waits for them, and re-layouts, local(): return (out[0:RUN], out[RUN:])  2.86 us

profile of v5, /device:TPU:1, one launch (start us, length us, event | category | flops | bytes accessed | tf_op | source)
XLA Modules:
  0.0 70.3 jit_solution(18147449163186000040)
XLA Ops:
  0.6 66.8 %step.1 = f32[136,256]{1,0:T(8,128)} custom-call(bf16[256,768]{1,0:T(8,128)(2,1)} %samples.1, f32[256,256]{1,0:T(8,128)} %targets.1, s32[128]{0:T(128)} %index.1, bf16[128,768]{1,0:T(8,128)(2,1)} %centers.1, f32[128,256]{1,0:T(8,128)} %weights.1, s32[1536]{0:T(1024)} %nys.1, f32[1536,128]{1,0:T(8,128)} %eig.1, f32[128]{0:T(128)} %coef.1), custom_call_target="tpu_custom_call" | custom-call | tf_op jit(solution)/shard_map/step/pallas_call | solution.py:523
  67.5 1.3 %slice.6 = f32[8,256]{1,0:T(8,128)} slice(f32[136,256]{1,0:T(8,128)} %step.1), slice={[0:8], [0:256]} | slice | bytes 16384 | tf_op jit(solution)/shard_map/slice | solution.py:547
  68.8 1.6 %slice.7 = f32[128,256]{1,0:T(8,128)} slice(f32[136,256]{1,0:T(8,128)} %step.1), slice={[8:136], [0:256]} | slice | bytes 262144 | tf_op jit(solution)/shard_map/slice | solution.py:547

commit v6 on v5

--- a/solution.py
+++ b/solution.py
@@ -465,12 +465,10 @@
     loop(8, lambda k: m_first(k, (z - k + NZ) % NZ).wait_recv(), 1)
     peers(lambda k: m_second(k, y).start())
     loop(8, lambda k: r_second(k, (z - k + NZ) % NZ).wait_recv(), 1)
-    loop(8, lambda k: m_second(k, (y - k + NY) % NY).wait_recv(), 1)
-    if STAGE == 4:
-        return drain(4)
 
     resid = jnp.concatenate([rall[pl.ds(2 * t, 2)].astype(F32).reshape(ROWS, 256) for t in slots], axis=0)
     resid_t = resid.T.astype(BF16)
+    loop(8, lambda k: m_second(k, (y - k + NY) % NY).wait_recv(), 1)
     m_slots = jnp.concatenate([mall[pl.ds(2 * t, 2)].reshape(ROWS, 128) for t in slots], axis=0)
     m1, m2, m3 = split3(m_slots)
     proj = dot(resid_t, m1) + dot(resid_t, m2) + dot(resid_t, m3)
@@ -498,9 +496,9 @@
     grad(x_prev)
     summed(x_next)
     near_half(0, 1).start()
-    grad(x)
     summed(x_prev)
     near_half(1, 0).start()
+    grad(x)
     far_half(0).wait_recv()
     gs[x_next, 0:128, :] += gx[2, 0:128, :]
     near_half(0, 0).start()

time: 70.5 us -> 70.5 us (level)
  no operation moved by 1% of the time
where the time goes in v6:
time: 70.5 us; the launch traced here: 70.3 us
  Pallas kernels  66.8 us (95%)
  local copies, waits for them, and re-layouts  2.86 us (4%)
    pallas_call x1, Pallas kernels, local(): pl.pallas_call(body, out_shape=jax.ShapeDtypeStruct((RUN + ROWS, 256), F3...  66.8 us
    slice x2, local copies, waits for them, and re-layouts, local(): return (out[0:RUN], out[RUN:])  2.86 us

profile of v6, /device:TPU:1, one launch (start us, length us, event | category | flops | bytes accessed | tf_op | source)
XLA Modules:
  0.0 70.3 jit_solution(4497396168599348487)
XLA Ops:
  0.6 66.8 %step.1 = f32[136,256]{1,0:T(8,128)} custom-call(bf16[256,768]{1,0:T(8,128)(2,1)} %samples.1, f32[256,256]{1,0:T(8,128)} %targets.1, s32[128]{0:T(128)} %index.1, bf16[128,768]{1,0:T(8,128)(2,1)} %centers.1, f32[128,256]{1,0:T(8,128)} %weights.1, s32[1536]{0:T(1024)} %nys.1, f32[1536,128]{1,0:T(8,128)} %eig.1, f32[128]{0:T(128)} %coef.1), custom_call_target="tpu_custom_call" | custom-call | tf_op jit(solution)/shard_map/step/pallas_call | solution.py:521
  67.4 1.3 %slice.6 = f32[8,256]{1,0:T(8,128)} slice(f32[136,256]{1,0:T(8,128)} %step.1), slice={[0:8], [0:256]} | slice | bytes 16384 | tf_op jit(solution)/shard_map/slice | solution.py:545
  68.7 1.6 %slice.7 = f32[128,256]{1,0:T(8,128)} slice(f32[136,256]{1,0:T(8,128)} %step.1), slice={[8:136], [0:256]} | slice | bytes 262144 | tf_op jit(solution)/shard_map/slice | solution.py:545
